TPU v7x, 256 devices: a whole 4x4x8 slice. The times are simulated.
256 devices in a mesh: slab: 64 (over x, z, core), tile: 4 (over y).
Axes of the slice: x: 4, y: 4, z: 8, core: 2. Of those that a mesh axis runs over, the one named last changes fastest.
Arguments:
- bricks: bfloat16 [64, 32, 32, 16, 256], P('slab', 'tile'), may hold values from -8 to 8
- send_list: int32 [64, 16, 2], P('slab', 'tile'), may hold values from -1 to 7, as said below
- sample_voxel: int32 [64, 512, 128], P('slab', 'tile'), may hold values from 0 to 3822, as said below
- sample_frac: float32 [64, 512, 3, 128], P('slab', 'tile'), may hold values from 0 to 1
- block_slot: int32 [64, 512], P('slab', 'tile'), may hold values from 0 to 7, as said below
- block_group: int32 [64, 512], P('slab', 'tile'), may hold values from -1 to 255, as said below
- density_weight: float32 [32], replicated, may hold values from -3 to 3
- background: float32 [32], replicated, may hold values from -4 to 4
- decode_weight: float32 [3, 32], replicated, may hold values from -2.1 to 2.1
- target: float32 [3, 4, 8192], P(None, 'tile', 'slab'), may hold values from 0 to 1
Outputs:
- rendered: float32 [3, 4, 8192], P(None, 'tile', 'slab')
- pixel_loss: float32 [4, 8192], P('tile', 'slab')
Inputs may be any that keep to these rules, and one draw needn't show every extreme that they name: `send_list`: entry [s, u * 4 + d, k] is the local brick that device (slab s, tile u) puts in send slot k for tile owner d of its slab, or -1 for an empty slot; the filled slots of a list come first, name distinct bricks and number 1 to 2; in every slab some owner gets 2 bricks from every source. `block_slot`: block b of owner (s, t) reads slot u * 2 + k, a filled slot of the list that tile u of slab s sends to t, where u = b // 32: a device's blocks come in 4 runs by source; every filled slot is read by some filled block of its run. `block_group`: -1 marks an empty block; in each run the filled blocks come first, all runs of a device hold the same number of filled blocks, at least 2, and a device's filled blocks have distinct groups; in every tile some slab's device is full. `sample_voxel`: x * 16 * 16 + y * 16 + z with x, y, z each at most 14.
All inputs are finite; a program needn't handle non-finite values.
Results may differ from a plain program's by a relative error of at most 0.0033.
Values may be sent and summed in bfloat16 or wider, within the bound.
No kernel may reach another device: no remote copies, remote signals or barrier semaphores. Data moves between devices by JAX's collectives and lax.ppermute only.
A program may use at most 64 MiB of HBM per device.

v0:
```python
import jax
import jax.numpy as jnp
from jax import lax
from jax.sharding import PartitionSpec as P

SPR = 4
GROUPS = 256


step_length = 0.02


def from_partner(block, axis, stride):
    count = lax.axis_size(axis)
    route = []
    for low in range(count):
        high = low | 1 << stride
        if high != low and high < count:
            route += [(low, high), (high, low)]
    return lax.ppermute(block, axis, route)


def axis_weights(line_index, cell_index, fraction):
    lower = jnp.where(line_index == cell_index[None, :], 1.0 - fraction[None, :], 0.0)
    upper = jnp.where(line_index == cell_index[None, :] + 1, fraction[None, :], 0.0)
    return lower + upper


def sample_bricks(brick_store, brick_ids, base_voxel, fractions):
    channels = brick_store.shape[1]
    brick_edge = brick_store.shape[2]

    def one_block(inputs):
        brick_id, voxel_row, frac_rows = inputs
        brick_cube = brick_store[brick_id]
        cell_x = voxel_row // (brick_edge * brick_edge)
        cell_y = voxel_row // brick_edge % brick_edge
        cell_z = voxel_row % brick_edge
        line_index = jnp.arange(brick_edge, dtype=jnp.int32)[:, None]
        weight_x = axis_weights(line_index, cell_x, frac_rows[0])
        weight_y = axis_weights(line_index, cell_y, frac_rows[1])
        weight_z = axis_weights(line_index, cell_z, frac_rows[2])
        plane_weights = (
            (weight_y[:, None, :] * weight_z[None, :, :])
            .reshape(brick_edge * brick_edge, -1)
            .astype(jnp.bfloat16)
        )
        plane_sums = jnp.dot(
            brick_cube.reshape(-1, brick_edge * brick_edge),
            plane_weights,
            preferred_element_type=jnp.float32,
        )
        plane_sums = plane_sums.reshape(channels, brick_edge, -1)
        return jnp.sum(weight_x[None] * plane_sums, axis=1).astype(jnp.bfloat16)

    return lax.map(one_block, (brick_ids, base_voxel, fractions), batch_size=8)


def shade_and_place(features, density_weight, groups):
    blocks = features.shape[0]
    channels = features.shape[1]
    sample_count = features.shape[2]
    rays = sample_count // SPR
    values = features.astype(jnp.float32)
    logits = jnp.einsum("c,bcs->bs", density_weight, values, precision=lax.Precision.HIGHEST)
    density = jax.nn.softplus(logits)
    opacity = 1.0 - jnp.exp(-step_length * density)
    steps_view = opacity.reshape(blocks, SPR, rays)
    through = jnp.cumprod(1.0 - steps_view, axis=1)
    before = jnp.concatenate([jnp.ones_like(through[:, :1]), through[:, :-1]], axis=1)
    sample_weight = (before * steps_view).reshape(blocks, sample_count)
    weighted = sample_weight[:, None, :] * values
    member = (groups[:, None] == jnp.arange(GROUPS, dtype=jnp.int32)[None, :]).astype(jnp.float32)
    spread = jnp.einsum("bg,bcs->cgs", member, weighted, precision=lax.Precision.HIGHEST)
    fold_table = (
        jnp.arange(sample_count, dtype=jnp.int32)[:, None] % rays
        == jnp.arange(rays, dtype=jnp.int32)[None, :]
    ).astype(jnp.float32)
    slab_feature = jnp.dot(
        spread.reshape(-1, sample_count),
        fold_table,
        precision=lax.Precision.HIGHEST,
        preferred_element_type=jnp.float32,
    )
    slab_feature = slab_feature.reshape(channels, GROUPS * rays)
    covered = jnp.sum(member, axis=0)
    slab_pass = jnp.dot(
        member.T,
        through[:, -1],
        precision=lax.Precision.HIGHEST,
        preferred_element_type=jnp.float32,
    )
    slab_pass = (slab_pass + (1.0 - covered)[:, None]).reshape(GROUPS * rays)
    return (slab_feature, slab_pass)


def on_device(
    bricks,
    send_list,
    sample_voxel,
    sample_frac,
    block_slot,
    block_group,
    density_weight,
    background,
    decode_weight,
    target,
):
    brick_store = bricks[0]
    send_lists = send_list[0]
    base_voxel = sample_voxel[0]
    fractions = sample_frac[0]
    slot_ids = block_slot[0]
    groups = block_group[0]
    tile_count = lax.axis_size("tile")
    slab_count = lax.axis_size("slab")
    capacity = send_lists.shape[1]
    last_brick = brick_store.shape[0] - 1
    chosen = jnp.clip(send_lists, 0, last_brick)
    outgoing = brick_store[chosen]
    received = lax.all_to_all(outgoing, "tile", split_axis=0, concat_axis=0, tiled=True)
    received = received.reshape((tile_count * capacity,) + brick_store.shape[1:])
    features = sample_bricks(received, slot_ids, base_voxel, fractions)
    slab_feature, slab_pass = shade_and_place(features, density_weight, groups)
    channels = slab_feature.shape[0]
    slab_feature = slab_feature.reshape(channels, slab_count, -1)
    slab_pass = slab_pass.reshape(1, slab_count, -1)
    front_feature = slab_feature
    front_pass = slab_pass
    position = lax.axis_index("slab")
    for bit_level in range(slab_count.bit_length() - 1):
        pair_feature = front_feature.reshape(channels, -1, 2, front_feature.shape[2])
        pair_pass = front_pass.reshape(1, -1, 2, front_pass.shape[2])
        nearer = position >> bit_level & 1 == 0
        kept_feature = jnp.where(nearer, pair_feature[:, :, 0], pair_feature[:, :, 1])
        kept_pass = jnp.where(nearer, pair_pass[:, :, 0], pair_pass[:, :, 1])
        sent_feature = jnp.where(nearer, pair_feature[:, :, 1], pair_feature[:, :, 0])
        sent_pass = jnp.where(nearer, pair_pass[:, :, 1], pair_pass[:, :, 0])
        got_feature, got_pass = from_partner((sent_feature, sent_pass), "slab", bit_level)
        front_feature = jnp.where(
            nearer, kept_feature + kept_pass * got_feature, got_feature + got_pass * kept_feature
        )
        front_pass = kept_pass * got_pass
    total_feature = front_feature[:, 0]
    total_pass = front_pass[:, 0]
    final_feature = total_feature + total_pass * background[:, None]
    logits = jnp.dot(
        decode_weight,
        final_feature,
        precision=lax.Precision.HIGHEST,
        preferred_element_type=jnp.float32,
    )
    colour = jax.nn.sigmoid(logits)
    difference = colour - target[:, 0]
    pixel_loss = jnp.sum(difference * difference, axis=0)
    return (colour[:, None, :], pixel_loss[None, :])


def solution(mesh):
    in_specs = (
        P("slab", "tile", None, None, None),
        P("slab", "tile", None),
        P("slab", "tile", None),
        P("slab", "tile", None, None),
        P("slab", "tile"),
        P("slab", "tile"),
        P(),
        P(),
        P(),
        P(None, "tile", "slab"),
    )
    out_specs = (P(None, "tile", "slab"), P("tile", "slab"))
    return jax.shard_map(
        on_device, mesh=mesh, in_specs=in_specs, out_specs=out_specs, check_vma=False
    )
```

profile of v0, /device:TPU:6, one launch (start us, length us, event | category | flops | bytes accessed | tf_op | source)
XLA Modules:
  0.0 271.3 jit_solution(4591659106195380444)
XLA Ops:
  4.3 3.7 %copy.18 = bf16[4,2,32,16,256]{4,2,3,1,0:T(8,128)(2,1)} copy(bf16[4,2,32,16,256]{4,3,2,1,0:T(8,128)(2,1)} %bitcast.332) | data formatting | bytes 4194304 | tf_op jit(solution)/shard_map/gather | solution.py:120
  8.0 4.6 %all-to-all-start = ((bf16[4,2,32,16,256]{4,2,3,1,0:T(8,128)(2,1)}), bf16[4,2,32,16,256]{4,2,3,1,0:T(8,128)(2,1)}, u32[]{:S(2)}, u32[]{:S(2)}) async-start(bf16[4,2,32,16,256]{4,2,3,1,0:T(8,128)(2,1)} %copy.18), calls=%async_computation | async-start | bytes 4194304 | tf_op jit(solution)/shard_map/all_to_all | solution.py:121
  14.0 25.3 %all-to-all-done = bf16[4,2,32,16,256]{4,2,3,1,0:T(8,128)(2,1)} async-done(((bf16[4,2,32,16,256]{4,2,3,1,0:T(8,128)(2,1)}), bf16[4,2,32,16,256]{4,2,3,1,0:T(8,128)(2,1)}, u32[]{:S(2)}, u32[]{:S(2)}) %all-to-all-start) | async-done | bytes 2097184 | tf_op jit(solution)/shard_map/all_to_all | solution.py:121
  39.2 153.2 %while.13 = (s32[]{:T(128)}, bf16[16,8,32,128]{3,2,1,0:T(8,128)(2,1)S(1)}, s32[16,8,128]{2,1,0:T(8,128)}, f32[16,8,3,128]{3,1,0,2:T(8,128)}, s32[16,8]{1,0:T(8,1...) while((s32[]{:T(128)}, bf16[16,8,32,128]{3,2,1,0:T(8,128)(2,1)S(1)}, s32[16,8,128]{2,1,0:T(8,128)}, ...), condition=%wide.region_2.3_spmd, body=%wide.region_0.2_spmd.sunk | while | flops 270275616 | bytes 12269865 | solution.py:56
  41.4 3.6 %gather_fusion = bf16[8,32,16,256]{3,1,2,0:T(8,128)(2,1)} fusion(bf16[8,32,16,256]{3,1,2,0:T(8,128)(2,1)} %get-tuple-element.257, s32[8]{0:T(128)S(1)} %shift-left_bitcast_fusion.2), kind=kCustom, calls=%fused_computation.clone.1 | custom fusion | bytes 4194432 | tf_op jit(solution)/shard_map/while/body/eval_jaxpr/vmap()/gather | solution.py:35
  51.0 3.6 %gather_fusion = bf16[8,32,16,256]{3,1,2,0:T(8,128)(2,1)} fusion(bf16[8,32,16,256]{3,1,2,0:T(8,128)(2,1)} %get-tuple-element.257, s32[8]{0:T(128)S(1)} %shift-left_bitcast_fusion.2), kind=kCustom, calls=%fused_computation.clone.1 | custom fusion | bytes 4194432 | tf_op jit(solution)/shard_map/while/body/eval_jaxpr/vmap()/gather | solution.py:35
  54.6 2.9 %copy.82 = bf16[8,32,16,256]{3,2,1,0:T(8,128)(2,1)S(1)} copy(bf16[8,32,16,256]{3,1,2,0:T(8,128)(2,1)} %gather_fusion) | data formatting | bytes 4194304 | tf_op jit(solution)/shard_map/while/body/eval_jaxpr/vmap()/gather | solution.py:35
  60.6 3.6 %gather_fusion = bf16[8,32,16,256]{3,1,2,0:T(8,128)(2,1)} fusion(bf16[8,32,16,256]{3,1,2,0:T(8,128)(2,1)} %get-tuple-element.257, s32[8]{0:T(128)S(1)} %shift-left_bitcast_fusion.2), kind=kCustom, calls=%fused_computation.clone.1 | custom fusion | bytes 4194432 | tf_op jit(solution)/shard_map/while/body/eval_jaxpr/vmap()/gather | solution.py:35
  70.1 3.6 %gather_fusion = bf16[8,32,16,256]{3,1,2,0:T(8,128)(2,1)} fusion(bf16[8,32,16,256]{3,1,2,0:T(8,128)(2,1)} %get-tuple-element.257, s32[8]{0:T(128)S(1)} %shift-left_bitcast_fusion.2), kind=kCustom, calls=%fused_computation.clone.1 | custom fusion | bytes 4194432 | tf_op jit(solution)/shard_map/while/body/eval_jaxpr/vmap()/gather | solution.py:35
  79.7 3.6 %gather_fusion = bf16[8,32,16,256]{3,1,2,0:T(8,128)(2,1)} fusion(bf16[8,32,16,256]{3,1,2,0:T(8,128)(2,1)} %get-tuple-element.257, s32[8]{0:T(128)S(1)} %shift-left_bitcast_fusion.2), kind=kCustom, calls=%fused_computation.clone.1 | custom fusion | bytes 4194432 | tf_op jit(solution)/shard_map/while/body/eval_jaxpr/vmap()/gather | solution.py:35
  89.3 3.6 %gather_fusion = bf16[8,32,16,256]{3,1,2,0:T(8,128)(2,1)} fusion(bf16[8,32,16,256]{3,1,2,0:T(8,128)(2,1)} %get-tuple-element.257, s32[8]{0:T(128)S(1)} %shift-left_bitcast_fusion.2), kind=kCustom, calls=%fused_computation.clone.1 | custom fusion | bytes 4194432 | tf_op jit(solution)/shard_map/while/body/eval_jaxpr/vmap()/gather | solution.py:35
  98.9 3.6 %gather_fusion = bf16[8,32,16,256]{3,1,2,0:T(8,128)(2,1)} fusion(bf16[8,32,16,256]{3,1,2,0:T(8,128)(2,1)} %get-tuple-element.257, s32[8]{0:T(128)S(1)} %shift-left_bitcast_fusion.2), kind=kCustom, calls=%fused_computation.clone.1 | custom fusion | bytes 4194432 | tf_op jit(solution)/shard_map/while/body/eval_jaxpr/vmap()/gather | solution.py:35
  108.5 3.6 %gather_fusion = bf16[8,32,16,256]{3,1,2,0:T(8,128)(2,1)} fusion(bf16[8,32,16,256]{3,1,2,0:T(8,128)(2,1)} %get-tuple-element.257, s32[8]{0:T(128)S(1)} %shift-left_bitcast_fusion.2), kind=kCustom, calls=%fused_computation.clone.1 | custom fusion | bytes 4194432 | tf_op jit(solution)/shard_map/while/body/eval_jaxpr/vmap()/gather | solution.py:35
  118.0 3.6 %gather_fusion = bf16[8,32,16,256]{3,1,2,0:T(8,128)(2,1)} fusion(bf16[8,32,16,256]{3,1,2,0:T(8,128)(2,1)} %get-tuple-element.257, s32[8]{0:T(128)S(1)} %shift-left_bitcast_fusion.2), kind=kCustom, calls=%fused_computation.clone.1 | custom fusion | bytes 4194432 | tf_op jit(solution)/shard_map/while/body/eval_jaxpr/vmap()/gather | solution.py:35
  127.6 3.6 %gather_fusion = bf16[8,32,16,256]{3,1,2,0:T(8,128)(2,1)} fusion(bf16[8,32,16,256]{3,1,2,0:T(8,128)(2,1)} %get-tuple-element.257, s32[8]{0:T(128)S(1)} %shift-left_bitcast_fusion.2), kind=kCustom, calls=%fused_computation.clone.1 | custom fusion | bytes 4194432 | tf_op jit(solution)/shard_map/while/body/eval_jaxpr/vmap()/gather | solution.py:35
  137.2 3.6 %gather_fusion = bf16[8,32,16,256]{3,1,2,0:T(8,128)(2,1)} fusion(bf16[8,32,16,256]{3,1,2,0:T(8,128)(2,1)} %get-tuple-element.257, s32[8]{0:T(128)S(1)} %shift-left_bitcast_fusion.2), kind=kCustom, calls=%fused_computation.clone.1 | custom fusion | bytes 4194432 | tf_op jit(solution)/shard_map/while/body/eval_jaxpr/vmap()/gather | solution.py:35
  146.8 3.6 %gather_fusion = bf16[8,32,16,256]{3,1,2,0:T(8,128)(2,1)} fusion(bf16[8,32,16,256]{3,1,2,0:T(8,128)(2,1)} %get-tuple-element.257, s32[8]{0:T(128)S(1)} %shift-left_bitcast_fusion.2), kind=kCustom, calls=%fused_computation.clone.1 | custom fusion | bytes 4194432 | tf_op jit(solution)/shard_map/while/body/eval_jaxpr/vmap()/gather | solution.py:35
  156.3 3.6 %gather_fusion = bf16[8,32,16,256]{3,1,2,0:T(8,128)(2,1)} fusion(bf16[8,32,16,256]{3,1,2,0:T(8,128)(2,1)} %get-tuple-element.257, s32[8]{0:T(128)S(1)} %shift-left_bitcast_fusion.2), kind=kCustom, calls=%fused_computation.clone.1 | custom fusion | bytes 4194432 | tf_op jit(solution)/shard_map/while/body/eval_jaxpr/vmap()/gather | solution.py:35
  165.9 3.6 %gather_fusion = bf16[8,32,16,256]{3,1,2,0:T(8,128)(2,1)} fusion(bf16[8,32,16,256]{3,1,2,0:T(8,128)(2,1)} %get-tuple-element.257, s32[8]{0:T(128)S(1)} %shift-left_bitcast_fusion.2), kind=kCustom, calls=%fused_computation.clone.1 | custom fusion | bytes 4194432 | tf_op jit(solution)/shard_map/while/body/eval_jaxpr/vmap()/gather | solution.py:35
  175.5 3.6 %gather_fusion = bf16[8,32,16,256]{3,1,2,0:T(8,128)(2,1)} fusion(bf16[8,32,16,256]{3,1,2,0:T(8,128)(2,1)} %get-tuple-element.257, s32[8]{0:T(128)S(1)} %shift-left_bitcast_fusion.2), kind=kCustom, calls=%fused_computation.clone.1 | custom fusion | bytes 4194432 | tf_op jit(solution)/shard_map/while/body/eval_jaxpr/vmap()/gather | solution.py:35
  185.1 3.6 %gather_fusion = bf16[8,32,16,256]{3,1,2,0:T(8,128)(2,1)} fusion(bf16[8,32,16,256]{3,1,2,0:T(8,128)(2,1)} %get-tuple-element.257, s32[8]{0:T(128)S(1)} %shift-left_bitcast_fusion.2), kind=kCustom, calls=%fused_computation.clone.1 | custom fusion | bytes 4194432 | tf_op jit(solution)/shard_map/while/body/eval_jaxpr/vmap()/gather | solution.py:35
  194.9 5.0 %convolution_bitcast_fusion = f32[32,256,128]{1,2,0:T(8,128)} fusion(bf16[128,32,128]{0,2,1:T(8,128)(2,1)} %copy.20, f32[128,128]{0,1:T(8,128)S(1)} %bitcast.347, s32[128]{0:T(128)S(1)} %bitcast.386), kind=kOutput, calls=%fused_computation.46 | convolution fusion | flops 1611694080 | bytes 5308928 | tf_op jit(solution)/shard_map/bg,bcs->cgs/dot_general | solution.py:74
  200.0 5.6 %copy.21 = f32[32,256,128]{2,1,0:T(8,128)} copy(f32[32,256,128]{1,2,0:T(8,128)} %convolution_bitcast_fusion) | data formatting | bytes 8388608 | tf_op jit(solution)/shard_map/bg,bcs->cgs/transpose | solution.py:74
  205.6 6.2 %fusion.30 = f32[8192,32]{1,0:T(8,128)} fusion(f32[8192,128]{1,0:T(8,128)} %bitcast.331, s32[128]{0:T(128)S(1)} %and_select_fusion), kind=kOutput, calls=%fused_computation.91 | convolution fusion | flops 402657280 | bytes 5243392 | tf_op jit(solution)/shard_map/dot_general | solution.py:79
  211.8 3.5 %reshape_reshape_reshape.6 = f32[32,32,2,128]{3,2,1,0:T(2,128)S(1)} reshape(f32[8192,32]{1,0:T(8,128)} %fusion.30) | data formatting | bytes 2097152 | tf_op jit(solution)/shard_map/reshape;reshape;reshape | solution.py:132
  215.3 2.9 %fusion.64 = (f32[32,32,1,128]{3,2,1,0:T(1,128)}, f32[32,32,1,128]{3,2,1,0:T(1,128)}, f32[32,32,1,128]{3,2,1,0:T(1,128)}) fusion(f32[32,32,2,128]{3,2,1,0:T(2,128)S(1)} %reshape_reshape_reshape.6, pred[]{:T(512)S(6)} %eq.190), kind=kLoop, calls=%fused_computation.153 | loop fusion | flops 131072 | bytes 2621441 | tf_op jit(solution)/shard_map/slice | solution.py:135
  224.1 3.4 %collective-permute-start.5 = (f32[1,8,128]{2,1,0:T(8,128)S(1)}, f32[1,8,128]{2,1,0:T(8,128)S(1)}, u32[]{:S(2)}, u32[]{:S(2)}) collective-permute-start(f32[1,8,128]{2,1,0:T(8,128)S(1)} %bitcast.381), channel_id=1, source_target_pairs={{0,16},{16,0},{4,20},{20,4},{8,24},{24,8},{12,28},{28,12},{32,48},... | collective-permute-start | bytes 12296 | tf_op jit(solution)/shard_map/ppermute | solution.py:20
  229.1 6.9 %collective-permute-start.7 = (f32[1,4,128]{2,1,0:T(4,128)S(1)}, f32[1,4,128]{2,1,0:T(4,128)S(1)}, u32[]{:S(2)}, u32[]{:S(2)}) collective-permute-start(f32[1,4,128]{2,1,0:T(4,128)S(1)} %bitcast.383), channel_id=1, source_target_pairs={{0,32},{32,0},{4,36},{36,4},{8,40},{40,8},{12,44},{44,12},{16,48},... | collective-permute-start | bytes 6152 | tf_op jit(solution)/shard_map/ppermute | solution.py:20
  239.7 4.4 %collective-permute-done.2 = f32[32,16,128]{2,0,1:T(8,128)S(1)} collective-permute-done((f32[32,16,128]{2,0,1:T(8,128)S(1)}, f32[32,16,128]{2,0,1:T(8,128)S(1)}, u32[]{:S(2)}, u32[]{:S(2)}) %collective-permute-start.2) | collective-permute-done | bytes 262176 | tf_op jit(solution)/shard_map/ppermute | solution.py:20
  246.1 6.2 %collective-permute-done.4 = f32[32,8,128]{2,0,1:T(8,128)S(1)} collective-permute-done((f32[32,8,128]{2,0,1:T(8,128)S(1)}, f32[32,8,128]{2,0,1:T(8,128)S(1)}, u32[]{:S(2)}, u32[]{:S(2)}) %collective-permute-start.4) | collective-permute-done | bytes 131104 | tf_op jit(solution)/shard_map/ppermute | solution.py:20
  252.5 8.1 %collective-permute-done.6 = f32[32,4,128]{2,0,1:T(8,128)S(1)} collective-permute-done((f32[32,4,128]{2,0,1:T(8,128)S(1)}, f32[32,4,128]{2,0,1:T(8,128)S(1)}, u32[]{:S(2)}, u32[]{:S(2)}) %collective-permute-start.6) | collective-permute-done | bytes 65568 | tf_op jit(solution)/shard_map/ppermute | solution.py:20
  266.7 3.4 %collective-permute-done.10 = f32[32,1,128]{2,0,1:T(8,128)S(1)} collective-permute-done((f32[32,1,128]{2,0,1:T(8,128)S(1)}, f32[32,1,128]{2,0,1:T(8,128)S(1)}, u32[]{:S(2)}, u32[]{:S(2)}) %collective-permute-start.10) | collective-permute-done | bytes 16416 | tf_op jit(solution)/shard_map/ppermute | solution.py:20
  (259 shorter events, 120.1 us)
Async XLA Ops:
  0.6 1.6 copy-start
  8.0 5.1 %copy-start.5 = (s32[1,128]{1,0:T(1,128)S(1)}, s32[1,128]{1,0:T(1,128)}, u32[]{:S(2)}) copy-start(s32[1,128]{1,0:T(1,128)} %param.16) | copy-start | bytes 1540
  8.0 5.9 %copy-start.2 = (s32[1,128]{1,0:T(1,128)S(1)}, s32[1,128]{1,0:T(1,128)}, u32[]{:S(2)}) copy-start(s32[1,128]{1,0:T(1,128)} %param.17) | copy-start | bytes 1540
  8.0 31.3 %all-to-all-start = ((bf16[4,2,32,16,256]{4,2,3,1,0:T(8,128)(2,1)}), bf16[4,2,32,16,256]{4,2,3,1,0:T(8,128)(2,1)}, u32[]{:S(2)}, u32[]{:S(2)}) async-start(bf16[4,2,32,16,256]{4,2,3,1,0:T(8,128)(2,1)} %copy.18), calls=%async_computation | async-start | bytes 4194304 | tf_op jit(solution)/shard_map/all_to_all | solution.py:121
  192.5 1.7 copy-start.1
  218.2 17.8 %collective-permute-start = (f32[32,32,128]{2,1,0:T(8,128)}, f32[32,32,128]{2,1,0:T(8,128)S(1)}, u32[]{:S(2)}, u32[]{:S(2)}) collective-permute-start(f32[32,32,128]{2,1,0:T(8,128)} %bitcast.35), channel_id=1, source_target_pairs={{0,4},{4,0},{8,12},{12,8},{16,20},{20,16},{24,28},{28,24},{32,36},... | collective-permute-start | bytes 1572872 | tf_op jit(solution)/shard_map/ppermute | solution.py:20
  218.7 1.6 collective-permute-start.1
  220.4 3.7 %collective-permute-start.3 = (f32[1,16,128]{2,1,0:T(8,128)S(1)}, f32[1,16,128]{2,1,0:T(8,128)S(1)}, u32[]{:S(2)}, u32[]{:S(2)}) collective-permute-start(f32[1,16,128]{2,1,0:T(8,128)S(1)} %bitcast.379), channel_id=1, source_target_pairs={{0,8},{8,0},{4,12},{12,4},{16,24},{24,16},{20,28},{28,20},{32,40},... | collective-permute-start | bytes 24584 | tf_op jit(solution)/shard_map/ppermute | solution.py:20
  224.1 4.9 %collective-permute-start.5 = (f32[1,8,128]{2,1,0:T(8,128)S(1)}, f32[1,8,128]{2,1,0:T(8,128)S(1)}, u32[]{:S(2)}, u32[]{:S(2)}) collective-permute-start(f32[1,8,128]{2,1,0:T(8,128)S(1)} %bitcast.381), channel_id=1, source_target_pairs={{0,16},{16,0},{4,20},{20,4},{8,24},{24,8},{12,28},{28,12},{32,48},... | collective-permute-start | bytes 12296 | tf_op jit(solution)/shard_map/ppermute | solution.py:20
  229.1 9.7 %collective-permute-start.7 = (f32[1,4,128]{2,1,0:T(4,128)S(1)}, f32[1,4,128]{2,1,0:T(4,128)S(1)}, u32[]{:S(2)}, u32[]{:S(2)}) collective-permute-start(f32[1,4,128]{2,1,0:T(4,128)S(1)} %bitcast.383), channel_id=1, source_target_pairs={{0,32},{32,0},{4,36},{36,4},{8,40},{40,8},{12,44},{44,12},{16,48},... | collective-permute-start | bytes 6152 | tf_op jit(solution)/shard_map/ppermute | solution.py:20
  237.3 32.8 %copy-start.3 = (f32[3,32]{1,0:T(4,128)S(1)}, f32[3,32]{1,0:T(4,128)}, u32[]{:S(2)}) copy-start(f32[3,32]{1,0:T(4,128)} %param.20) | copy-start | bytes 1156
  237.3 32.8 %copy-start.4 = (f32[3,1,128]{2,1,0:T(1,128)S(1)}, f32[3,1,128]{2,1,0:T(1,128)}, u32[]{:S(2)}) copy-start(f32[3,1,128]{2,1,0:T(1,128)} %param.21) | copy-start | bytes 4612
  237.3 32.8 %copy-start.6 = (f32[32]{0:T(128)S(1)}, f32[32]{0:T(128)}, u32[]{:S(2)}) copy-start(f32[32]{0:T(128)} %param.19) | copy-start | bytes 388
  237.6 6.5 %collective-permute-start.2 = (f32[32,16,128]{2,0,1:T(8,128)S(1)}, f32[32,16,128]{2,0,1:T(8,128)S(1)}, u32[]{:S(2)}, u32[]{:S(2)}) collective-permute-start(f32[32,16,128]{2,0,1:T(8,128)S(1)} %select_bitcast_fusion), channel_id=1, source_target_pairs={{0,8},{8,0},{4,12},{12,4},{16,24},{24,16},{20,28},{28,20},{32,40},... | collective-permute-start | bytes 786440 | tf_op jit(solution)/shard_map/ppermute | solution.py:20
  238.8 13.7 %collective-permute-start.9 = (f32[1,2,128]{2,1,0:T(2,128)S(1)}, f32[1,2,128]{2,1,0:T(2,128)S(1)}, u32[]{:S(2)}, u32[]{:S(2)}) collective-permute-start(f32[1,2,128]{2,1,0:T(2,128)S(1)} %bitcast.384), channel_id=1, source_target_pairs={{0,64},{64,0},{4,68},{68,4},{8,72},{72,8},{12,76},{76,12},{16,80},... | collective-permute-start | bytes 3080 | tf_op jit(solution)/shard_map/ppermute | solution.py:20
  244.2 8.1 %collective-permute-start.4 = (f32[32,8,128]{2,0,1:T(8,128)S(1)}, f32[32,8,128]{2,0,1:T(8,128)S(1)}, u32[]{:S(2)}, u32[]{:S(2)}) collective-permute-start(f32[32,8,128]{2,0,1:T(8,128)S(1)} %select_bitcast_fusion.1), channel_id=1, source_target_pairs={{0,16},{16,0},{4,20},{20,4},{8,24},{24,8},{12,28},{28,12},{32,48},... | collective-permute-start | bytes 393224 | tf_op jit(solution)/shard_map/ppermute | solution.py:20
  252.4 8.3 %collective-permute-start.6 = (f32[32,4,128]{2,0,1:T(8,128)S(1)}, f32[32,4,128]{2,0,1:T(8,128)S(1)}, u32[]{:S(2)}, u32[]{:S(2)}) collective-permute-start(f32[32,4,128]{2,0,1:T(8,128)S(1)} %select_bitcast_fusion.2), channel_id=1, source_target_pairs={{0,32},{32,0},{4,36},{36,4},{8,40},{40,8},{12,44},{44,12},{16,48},... | collective-permute-start | bytes 196616 | tf_op jit(solution)/shard_map/ppermute | solution.py:20
  260.7 4.0 %collective-permute-start.8 = (f32[32,2,128]{2,0,1:T(8,128)S(1)}, f32[32,2,128]{2,0,1:T(8,128)S(1)}, u32[]{:S(2)}, u32[]{:S(2)}) collective-permute-start(f32[32,2,128]{2,0,1:T(8,128)S(1)} %select_bitcast_fusion.4), channel_id=1, source_target_pairs={{0,64},{64,0},{4,68},{68,4},{8,72},{72,8},{12,76},{76,12},{16,80},... | collective-permute-start | bytes 98312 | tf_op jit(solution)/shard_map/ppermute | solution.py:20
  261.6 5.1 %collective-permute-start.11 = (f32[1,1,128]{2,1,0:T(1,128)S(1)}, f32[1,1,128]{2,1,0:T(1,128)S(1)}, u32[]{:S(2)}, u32[]{:S(2)}) collective-permute-start(f32[1,1,128]{2,1,0:T(1,128)S(1)} %get-tuple-element.168), channel_id=1, source_target_pairs={{0,128},{128,0},{4,132},{132,4},{8,136},{136,8},{12,140},{140,12},... | collective-permute-start | bytes 1544 | tf_op jit(solution)/shard_map/ppermute | solution.py:20
  264.7 5.3 %collective-permute-start.10 = (f32[32,1,128]{2,0,1:T(8,128)S(1)}, f32[32,1,128]{2,0,1:T(8,128)S(1)}, u32[]{:S(2)}, u32[]{:S(2)}) collective-permute-start(f32[32,1,128]{2,0,1:T(8,128)S(1)} %select_bitcast_fusion.5), channel_id=1, source_target_pairs={{0,128},{128,0},{4,132},{132,4},{8,136},{136,8},{12,140},{140,12},... | collective-permute-start | bytes 49160 | tf_op jit(solution)/shard_map/ppermute | solution.py:20
where the time goes:
time: 275 us; the launch traced here: 271 us
  local copies, waits for them, and re-layouts  134 us (49%)
  waiting for transfers between devices  54.2 us (20%)
  other arithmetic  31.4 us (11%)
  starting transfers between devices  25 us (9%)
  matrix products  25 us (9%)
    gather x32, local copies, waits for them, and re-layouts, one_block(): brick_cube = brick_store[brick_id]  103 us
    ppermute x12, waiting for transfers between devices, from_partner(): return lax.ppermute(block, axis, route)  28.9 us
    all_to_all x1, waiting for transfers between devices, on_device(): lax.all_to_all(outgoing, 'tile', split_axis=0, concat_axis=0, tiled=True)  25.3 us
    add x32, other arithmetic, axis_weights(): cell_index[None, :] + 1  22.5 us
    ppermute x12, starting transfers between devices, from_partner(): return lax.ppermute(block, axis, route)  20.4 us
    dot_general x16, matrix products, one_block(): jnp.dot(brick_cube.reshape(-1, brick_edge * brick_edge), plane_weights, p...  12.2 us
    squeeze x16, local copies, waits for them, and re-layouts, sample_bricks(): return lax.map(one_block, (brick_ids, base_voxel, fractions), batch_size=8)  11.4 us
    dot_general x1, matrix products, shade_and_place(): jnp.dot(spread.reshape(-1, sample_count), fold_table, precision=lax.Preci...  6.19 us
  transfers between devices with their start and end apart: 13, of which 10 were waited for; matrix products, arithmetic and copies ran while one was open for 1% of the time, Pallas kernels for 0%

commit v1 on v0

v1 whole, which is shorter than its diff:
```python
import jax
import jax.numpy as jnp
from jax import lax
from jax.experimental import pallas as pl
from jax.experimental.pallas import tpu as pltpu
from jax.sharding import PartitionSpec as P

SPR = 4
GROUPS = 256
VALUES = 4

step_length = 0.02
f32 = jnp.float32
bf16 = jnp.bfloat16


def whole(space):
    return pl.BlockSpec(memory_space=space)


def decode_kernel(send_ref, density_ref, decode_ref, bricks_ref, out_ref, buffer, sems):
    slots = out_ref.shape[0]
    capacity = send_ref.shape[1]
    last_brick = bricks_ref.shape[1] - 1
    channels, edge, plane = bricks_ref.shape[2:]

    def copy_of(slot):
        brick = jnp.clip(send_ref[0, slot % capacity, slot // capacity], 0, last_brick)
        return pltpu.make_async_copy(bricks_ref.at[0, brick], buffer.at[slot], sems.at[slot])

    for slot in range(slots):
        copy_of(slot).start()

    def one_slot(slot, carry):
        copy_of(slot).wait()
        sums = [jnp.zeros((edge, plane), f32) for _ in range(VALUES)]
        for c in range(channels):
            values = buffer[slot, c].astype(f32)
            weights = [density_ref[c]] + [decode_ref[k, c] for k in range(VALUES - 1)]
            sums = [total + weight * values for total, weight in zip(sums, weights)]
        for k in range(VALUES):
            out_ref[slot, k * edge : (k + 1) * edge, :] = sums[k].astype(bf16)
        return carry

    lax.fori_loop(0, slots, one_slot, 0)


def decode_bricks(send_list, density_weight, decode_weight, bricks):
    slots = send_list.shape[1] * send_list.shape[2]
    channels, edge, plane = bricks.shape[2:]
    return pl.pallas_call(
        decode_kernel,
        out_shape=jax.ShapeDtypeStruct((slots, VALUES * edge, plane), bf16),
        in_specs=[whole(pltpu.SMEM)] * 3 + [whole(pltpu.HBM)],
        out_specs=whole(pltpu.VMEM),
        scratch_shapes=[
            pltpu.VMEM((slots, channels, edge, plane), bf16),
            pltpu.SemaphoreType.DMA((slots,)),
        ],
        compiler_params=pltpu.CompilerParams(vmem_limit_bytes=8 << 20),
        name="decode_bricks",
    )(send_list.transpose(0, 2, 1), density_weight, decode_weight, bricks)


def hat(position, line):
    return jnp.maximum(1.0 - jnp.abs(position - line), 0.0)


def sum_rows(parts):
    row = lax.broadcasted_iota(jnp.int32, parts[0].shape, 0)
    halves = []
    for j in range(4):
        low, high = parts[j], parts[j + 4]
        kept = jnp.where(row < 4, low, high)
        moved = jnp.where(row < 4, high, low)
        both = kept + pltpu.roll(moved, 4, 0)
        both = both + pltpu.roll(both, 1 if j & 1 else 7, 0)
        both = both + pltpu.roll(both, 2 if j & 2 else 6, 0)
        halves.append(both)
    odd = (row & 1) == 1
    pair0 = jnp.where(odd, halves[1], halves[0])
    pair1 = jnp.where(odd, halves[3], halves[2])
    return jnp.where((row & 2) == 2, pair1, pair0)


def sample_kernel(slot_ref, planes_ref, voxel_ref, frac_ref, group_ref, column_ref, out_ref, shaded):
    blocks, samples = voxel_ref.shape[1:]
    edge = planes_ref.shape[1] // VALUES
    rays = samples // SPR
    batch = 8
    line = lax.broadcasted_iota(jnp.int32, (edge, samples), 0).astype(f32)
    lane = lax.broadcasted_iota(jnp.int32, (batch, samples), 1)
    quarter = lane // rays

    def one_batch(step, carry):
        first = pl.multiple_of(step * batch, batch)
        voxel = voxel_ref[0, pl.ds(first, batch), :]
        cells = (voxel // (edge * edge), voxel // edge % edge, voxel % edge)
        at_x, at_y, at_z = [
            cell.astype(f32) + frac_ref[0, axis, pl.ds(first, batch), :] for axis, cell in enumerate(cells)
        ]
        parts = []
        for j in range(batch):
            weight_x = hat(at_x[j : j + 1], line)
            weight_y = hat(at_y[j : j + 1], line)
            weight_z = hat(at_z[j : j + 1], line)
            plane_weights = (
                (weight_y[:, None, :] * weight_z[None, :, :]).reshape(edge * edge, samples).astype(bf16)
            )
            sums = jnp.dot(
                planes_ref[slot_ref[0, first + j]], plane_weights, preferred_element_type=f32
            )
            sums = sums.reshape(VALUES, edge // 8, 8, samples)
            parts.append(jnp.sum(sums * weight_x.reshape(1, edge // 8, 8, samples), axis=1))
        logit, red, green, blue = [sum_rows([part[k] for part in parts]) for k in range(VALUES)]
        depth = step_length * (jnp.maximum(logit, 0.0) + jnp.log1p(jnp.exp(-jnp.abs(logit))))
        before = jnp.zeros_like(depth)
        total = depth
        for d in range(1, SPR):
            moved = pltpu.roll(depth, d * rays, 1)
            before = before + jnp.where(quarter >= d, moved, 0.0)
            total = total + moved
        weight = jnp.exp(-before) * (1.0 - jnp.exp(-depth))
        place = quarter == column_ref[pl.ds(first, batch), :] % SPR
        for k, value in enumerate((red, green, blue)):
            value = weight * value
            value = value + pltpu.roll(value, 2 * rays, 1)
            value = value + pltpu.roll(value, rays, 1)
            shaded[k, pl.ds(first, batch), :] = jnp.where(place, value, 0.0)
        shaded[VALUES - 1, pl.ds(first, batch), :] = jnp.where(place, total, 0.0)
        return carry

    lax.fori_loop(0, blocks // batch, one_batch, 0)
    rows = out_ref.shape[0]
    row = lax.broadcasted_iota(jnp.int32, (rows, blocks), 0)
    home = group_ref[...] // SPR
    chosen = [
        ((home == row // VALUES) & (row % VALUES == k)).astype(f32).astype(bf16) for k in range(VALUES)
    ]
    placed = jnp.dot(
        jnp.concatenate(chosen, axis=1),
        shaded[...].astype(bf16).reshape(VALUES * blocks, samples),
        preferred_element_type=f32,
    )
    out_ref[...] = placed.astype(bf16)


def sample_and_place(block_slot, planes, sample_voxel, sample_frac, block_group):
    blocks, samples = sample_voxel.shape[1:]
    return pl.pallas_call(
        sample_kernel,
        out_shape=jax.ShapeDtypeStruct((GROUPS // SPR * VALUES, samples), bf16),
        in_specs=[whole(pltpu.SMEM)] + [whole(pltpu.VMEM)] * 5,
        out_specs=whole(pltpu.VMEM),
        scratch_shapes=[pltpu.VMEM((VALUES, blocks, samples), f32)],
        compiler_params=pltpu.CompilerParams(vmem_limit_bytes=8 << 20),
        name="sample_and_place",
    )(
        block_slot,
        planes,
        sample_voxel,
        sample_frac.transpose(0, 2, 1, 3),
        block_group,
        block_group.reshape(blocks, 1),
    )


def composite_kernel(got_ref, background_ref, decode_ref, target_ref, colour_ref, loss_ref):
    rows, rays = got_ref.shape
    got = got_ref[...]
    here = lax.broadcasted_iota(jnp.int32, (rows, rows), 0) // VALUES
    there = lax.broadcasted_iota(jnp.int32, (rows, rows), 1)
    nearer = (there // VALUES < here) & (there % VALUES == VALUES - 1)
    depth = jnp.dot(nearer.astype(f32).astype(bf16), got, preferred_element_type=f32)
    is_depth = lax.broadcasted_iota(jnp.int32, (rows, rays), 0) % VALUES == VALUES - 1
    terms = got.astype(f32) * jnp.where(is_depth, 1.0, jnp.exp(-depth))
    total = jnp.sum(terms.reshape(rows // 8, 8, rays), axis=0)
    total = total + pltpu.roll(total, VALUES, 0)
    behind = jnp.sum(decode_ref[...] * background_ref[...], axis=1, keepdims=True)
    logits = total[0:3] + jnp.exp(-total[3:4]) * behind
    colour = jax.nn.sigmoid(logits)
    difference = colour - target_ref[:, 0, :]
    colour_ref[:, 0, :] = colour
    loss_ref[...] = jnp.sum(difference * difference, axis=0, keepdims=True)


def composite(got, background, decode_weight, target):
    rays = got.shape[1]
    return pl.pallas_call(
        composite_kernel,
        out_shape=(
            jax.ShapeDtypeStruct((3, 1, rays), f32),
            jax.ShapeDtypeStruct((1, rays), f32),
        ),
        in_specs=[whole(pltpu.VMEM)] * 4,
        out_specs=(whole(pltpu.VMEM), whole(pltpu.VMEM)),
        compiler_params=pltpu.CompilerParams(vmem_limit_bytes=8 << 20),
        name="composite",
    )(got, background.reshape(1, -1), decode_weight, target)


def on_device(
    bricks,
    send_list,
    sample_voxel,
    sample_frac,
    block_slot,
    block_group,
    density_weight,
    background,
    decode_weight,
    target,
):
    slab_count = lax.axis_size("slab")
    planes = decode_bricks(send_list, density_weight, decode_weight, bricks)
    planes = lax.all_to_all(planes, "tile", split_axis=0, concat_axis=0, tiled=True)
    placed = sample_and_place(block_slot, planes, sample_voxel, sample_frac, block_group)
    placed = placed.reshape(slab_count, VALUES, placed.shape[1])
    got = lax.all_to_all(placed, "slab", split_axis=0, concat_axis=0, tiled=True)
    return composite(got.reshape(-1, got.shape[2]), background, decode_weight, target)


def solution(mesh):
    in_specs = (
        P("slab", "tile", None, None, None),
        P("slab", "tile", None),
        P("slab", "tile", None),
        P("slab", "tile", None, None),
        P("slab", "tile"),
        P("slab", "tile"),
        P(),
        P(),
        P(),
        P(None, "tile", "slab"),
    )
    out_specs = (P(None, "tile", "slab"), P("tile", "slab"))
    return jax.shard_map(
        on_device, mesh=mesh, in_specs=in_specs, out_specs=out_specs, check_vma=False
    )
```

time: 275 us -> 51.3 us (0.19)
  the two profiles are of different devices: /device:TPU:6 before, /device:TPU:1 now
where the time goes in v1:
time: 51.3 us; the launch traced here: 51 us
  blocking collectives  23.1 us (45%)
  Pallas kernels  13 us (25%)
  waiting for transfers between devices  5.41 us (11%)
  starting transfers between devices  5.01 us (10%)
  local copies, waits for them, and re-layouts  3.76 us (7%)
  between operations  0.7 us (1%)
    all_to_all x1, blocking collectives, on_device(): lax.all_to_all(placed, 'slab', split_axis=0, concat_axis=0, tiled=True)  23.1 us
    pallas_call x1, Pallas kernels, sample_and_place(): pl.pallas_call(sample_kernel, out_shape=jax.ShapeDtypeStruct((GROUPS // S...  9.16 us
    all_to_all x1, waiting for transfers between devices, on_device(): lax.all_to_all(planes, 'tile', split_axis=0, concat_axis=0, tiled=True)  5.41 us
    all_to_all x1, starting transfers between devices, on_device(): lax.all_to_all(planes, 'tile', split_axis=0, concat_axis=0, tiled=True)  5.01 us
    unnamed x22, local copies, waits for them, and re-layouts  3.64 us
    pallas_call x1, Pallas kernels, decode_bricks(): pl.pallas_call(decode_kernel, out_shape=jax.ShapeDtypeStruct((slots, VALU...  3.04 us
  transfers between devices with their start and end apart: 1, of which 1 were waited for; matrix products, arithmetic and copies ran while one was open for 0% of the time, Pallas kernels for 0%

profile of v1, /device:TPU:1, one launch (start us, length us, event | category | flops | bytes accessed | tf_op | source)
XLA Modules:
  0.0 51.0 jit_solution(8946695250339033752)
XLA Ops:
  0.6 0.0 copy-start.5
  0.6 0.0 copy-start.8
  0.7 0.0 copy-start.9
  0.7 0.0 copy-start
  0.7 1.6 %copy-done = bf16[1,8,32,16,256]{4,3,2,1,0:T(8,128)(2,1)S(1)} copy-done((bf16[1,8,32,16,256]{4,3,2,1,0:T(8,128)(2,1)S(1)}, bf16[1,8,32,16,256]{4,3,2,1,0:T(8,128)(2,1)}, u32[]{:S(2)}) %copy-start) | copy-done | bytes 2097176
  2.3 0.0 copy-start.3
  2.3 0.7 %copy-done.3 = f32[3,32]{1,0:T(4,128)S(1)} copy-done((f32[3,32]{1,0:T(4,128)S(1)}, f32[3,32]{1,0:T(4,128)}, u32[]{:S(2)}) %copy-start.3) | copy-done | bytes 408
  3.0 0.0 copy-start.7
  3.0 0.7 %copy-done.7 = s32[1,4,2]{1,2,0:T(2,128)S(1)} copy-done((s32[1,4,2]{1,2,0:T(2,128)S(1)}, s32[1,4,2]{1,2,0:T(2,128)}, u32[]{:S(2)}) %copy-start.7) | copy-done | bytes 56
  3.6 0.0 copy-start.10
  3.6 0.7 %copy-done.10 = f32[32]{0:T(128)S(1)} copy-done((f32[32]{0:T(128)S(1)}, f32[32]{0:T(128)}, u32[]{:S(2)}) %copy-start.10) | copy-done | bytes 152
  4.3 0.0 copy-start.1
  4.3 0.0 copy-start.2
  4.3 0.0 copy-start.4
  4.3 0.0 copy-start.6
  4.3 3.0 %decode_bricks.1 = bf16[8,64,256]{2,1,0:T(8,128)(2,1)} custom-call(s32[1,2,4]{2,1,0:T(2,128)S(1)} %bitcast.10, f32[32]{0:T(128)S(1)} %copy-done.10, f32[3,32]{1,0:T(4,128)S(1)} %copy-done.3, bf16[1,8,32,16,256]{4,3,2,1,0:T(8,128)(2,1)S(1)} %copy-done), custom_call_target="tpu_custom_call" | custom-call | tf_op jit(solution)/shard_map/decode_bricks/pallas_call | solution.py:51
  7.4 5.0 %all-to-all-start = ((bf16[8,64,256]{2,1,0:T(8,128)(2,1)}), bf16[8,64,256]{2,1,0:T(8,128)(2,1)S(1)}, u32[]{:S(2)}, u32[]{:S(2)}) async-start(bf16[8,64,256]{2,1,0:T(8,128)(2,1)} %decode_bricks.1), calls=%async_computation | async-start | bytes 524288 | tf_op jit(solution)/shard_map/all_to_all | solution.py:216
  12.4 0.0 copy-done.5
  12.4 0.1 copy.12.column_ref
  12.5 5.4 %all-to-all-done.planes_ref = bf16[8,64,256]{2,1,0:T(8,128)(2,1)S(1)} async-done(((bf16[8,64,256]{2,1,0:T(8,128)(2,1)}), bf16[8,64,256]{2,1,0:T(8,128)(2,1)S(1)}, u32[]{:S(2)}, u32[]{:S(2)}) %all-to-all-start) | async-done | bytes 262176 | tf_op jit(solution)/shard_map/all_to_all | solution.py:216
  17.9 0.0 copy-done.8
  17.9 0.0 copy-done.1
  17.9 0.0 copy-done.2
  17.9 9.2 %sample_and_place.1 = bf16[256,128]{1,0:T(8,128)(2,1)S(1)} custom-call(s32[1,128]{1,0:T(1,128)S(1)} %copy-done.8, bf16[8,64,256]{2,1,0:T(8,128)(2,1)S(1)} %all-to-all-done.planes_ref, s32[1,128,128]{2,1,0:T(8,128)S(1)} %copy-done.2, f32[1,3,128,128]{3,2,1,0:T(8,128)S(1)} %bitcast.8, s32[1,128]{1,0:T(1,128)S(1)} %copy-done.5, s32[128,1]{1,0:T(8,128)S(1)} %copy.12.column_ref), custom_call_target="tpu_custom_call" | custom-call | tf_op jit(solution)/shard_map/sample_and_place/pallas_call | solution.py:150
  27.1 23.1 %all_to_all.10 = bf16[64,4,128]{2,1,0:T(4,128)(2,1)S(1)} all-to-all(bf16[64,4,128]{2,1,0:T(4,128)(2,1)S(1)} %bitcast.6), channel_id=1, replica_groups=mesh['slab'=64,'tile'=4] {'slab'}, dimensions={0} | all-to-all | bytes 131072 | tf_op jit(solution)/shard_map/all_to_all | solution.py:219
  50.2 0.0 copy-done.9
  50.2 0.0 copy-done.4
  50.2 0.0 copy-done.6
  50.2 0.8 %composite.1 = (f32[3,1,128]{2,1,0:T(1,128)}, f32[1,128]{1,0:T(1,128)}) custom-call(bf16[256,128]{1,0:T(8,128)(2,1)S(1)} %bitcast.7, f32[1,32]{1,0:T(1,128)S(1)} %bitcast.11, f32[3,32]{1,0:T(4,128)S(1)} %copy-done.4, f32[3,1,128]{2,1,0:T(1,128)S(1)} %copy-done.6), custom_call_target="tpu_custom_call" | custom-call | tf_op jit(solution)/shard_map/composite/pallas_call | solution.py:189
Async XLA Ops:
  0.6 11.7 %copy-start.5 = (s32[1,128]{1,0:T(1,128)S(1)}, s32[1,128]{1,0:T(1,128)}, u32[]{:S(2)}) copy-start(s32[1,128]{1,0:T(1,128)} %group_ref.1) | copy-start | bytes 1540
  0.6 17.3 %copy-start.8 = (s32[1,128]{1,0:T(1,128)S(1)}, s32[1,128]{1,0:T(1,128)}, u32[]{:S(2)}) copy-start(s32[1,128]{1,0:T(1,128)} %slot_ref.1) | copy-start | bytes 1540
  0.7 49.6 %copy-start.9 = (f32[32]{0:T(128)S(1)}, f32[32]{0:T(128)}, u32[]{:S(2)}) copy-start(f32[32]{0:T(128)} %param.17) | copy-start | bytes 388
  0.7 1.6 %copy-start = (bf16[1,8,32,16,256]{4,3,2,1,0:T(8,128)(2,1)S(1)}, bf16[1,8,32,16,256]{4,3,2,1,0:T(8,128)(2,1)}, u32[]{:S(2)}) copy-start(bf16[1,8,32,16,256]{4,3,2,1,0:T(8,128)(2,1)} %bricks_ref.1) | copy-start | bytes 6291460
  2.3 0.7 %copy-start.3 = (f32[3,32]{1,0:T(4,128)S(1)}, f32[3,32]{1,0:T(4,128)}, u32[]{:S(2)}) copy-start(f32[3,32]{1,0:T(4,128)} %decode_ref.3) | copy-start | bytes 1156
  3.0 0.7 %copy-start.7 = (s32[1,4,2]{1,2,0:T(2,128)S(1)}, s32[1,4,2]{1,2,0:T(2,128)}, u32[]{:S(2)}) copy-start(s32[1,4,2]{1,2,0:T(2,128)} %param.11) | copy-start | bytes 100
  3.6 0.7 %copy-start.10 = (f32[32]{0:T(128)S(1)}, f32[32]{0:T(128)}, u32[]{:S(2)}) copy-start(f32[32]{0:T(128)} %density_ref.1) | copy-start | bytes 388
  4.3 13.6 %copy-start.1 = (f32[1,128,3,128]{3,1,2,0:T(8,128)S(1)}, f32[1,128,3,128]{3,1,2,0:T(8,128)}, u32[]{:S(2)}) copy-start(f32[1,128,3,128]{3,1,2,0:T(8,128)} %param.13) | copy-start | bytes 589828
  4.3 13.6 %copy-start.2 = (s32[1,128,128]{2,1,0:T(8,128)S(1)}, s32[1,128,128]{2,1,0:T(8,128)}, u32[]{:S(2)}) copy-start(s32[1,128,128]{2,1,0:T(8,128)} %voxel_ref.1) | copy-start | bytes 196612
  4.3 45.9 %copy-start.4 = (f32[3,32]{1,0:T(4,128)S(1)}, f32[3,32]{1,0:T(4,128)}, u32[]{:S(2)}) copy-start(f32[3,32]{1,0:T(4,128)} %decode_ref.3) | copy-start | bytes 1156
  4.3 45.9 %copy-start.6 = (f32[3,1,128]{2,1,0:T(1,128)S(1)}, f32[3,1,128]{2,1,0:T(1,128)}, u32[]{:S(2)}) copy-start(f32[3,1,128]{2,1,0:T(1,128)} %target_ref.1) | copy-start | bytes 4612
  7.4 10.5 %all-to-all-start = ((bf16[8,64,256]{2,1,0:T(8,128)(2,1)}), bf16[8,64,256]{2,1,0:T(8,128)(2,1)S(1)}, u32[]{:S(2)}, u32[]{:S(2)}) async-start(bf16[8,64,256]{2,1,0:T(8,128)(2,1)} %decode_bricks.1), calls=%async_computation | async-start | bytes 524288 | tf_op jit(solution)/shard_map/all_to_all | solution.py:216

commit v2 on v1

v2 whole, which is shorter than its diff:
```python
import functools

import jax
import jax.numpy as jnp
from jax import lax
from jax.experimental import pallas as pl
from jax.experimental.pallas import tpu as pltpu
from jax.sharding import PartitionSpec as P

SPR = 4
GROUPS = 256
VALUES = 4

step_length = 0.02
f32 = jnp.float32
bf16 = jnp.bfloat16


def whole(space):
    return pl.BlockSpec(memory_space=space)


def decode_kernel(send_ref, density_ref, decode_ref, bricks_ref, *refs):
    tiles = len(refs) - 6
    outs = refs[:tiles]
    send, density, decode, buffer, decoded, sems = refs[tiles:]
    capacity = outs[0].shape[0]
    bricks, channels, edge, plane = bricks_ref.shape[1:]
    small = [
        pltpu.make_async_copy(source, target, sems.at[bricks + i])
        for i, (source, target) in enumerate(
            ((send_ref, send), (density_ref, density), (decode_ref, decode))
        )
    ]
    large = [
        pltpu.make_async_copy(bricks_ref.at[0, brick], buffer.at[brick], sems.at[brick])
        for brick in range(bricks)
    ]
    for copy in small + large:
        copy.start()
    for copy in small:
        copy.wait()

    def one_brick(brick, carry):
        pltpu.make_async_copy(bricks_ref.at[0, brick], buffer.at[brick], sems.at[brick]).wait()
        sums = [jnp.zeros((edge, plane), f32) for _ in range(VALUES)]
        for c in range(channels):
            values = buffer[brick, c].astype(f32)
            weights = [density[c]] + [decode[k, c] for k in range(VALUES - 1)]
            sums = [total + weight * values for total, weight in zip(sums, weights)]
        for k in range(VALUES):
            decoded[brick, k * edge : (k + 1) * edge, :] = sums[k].astype(bf16)
        return carry

    lax.fori_loop(0, bricks, one_brick, 0)
    here = lax.axis_index("tile")
    for r in range(tiles):
        owner = lax.rem(here + r, tiles)
        for slot in range(capacity):
            outs[r][slot] = decoded[jnp.clip(send[0, slot, owner], 0, bricks - 1)]


def decode_bricks(send_list, density_weight, decode_weight, bricks):
    tiles, capacity = send_list.shape[1:]
    send_list = send_list.transpose(0, 2, 1)
    count, channels, edge, plane = bricks.shape[1:]
    return pl.pallas_call(
        decode_kernel,
        out_shape=(jax.ShapeDtypeStruct((capacity, VALUES * edge, plane), bf16),) * tiles,
        in_specs=[whole(pltpu.HBM)] * 4,
        out_specs=(whole(pltpu.VMEM),) * tiles,
        scratch_shapes=[
            pltpu.SMEM(send_list.shape, jnp.int32),
            pltpu.SMEM(density_weight.shape, f32),
            pltpu.SMEM(decode_weight.shape, f32),
            pltpu.VMEM((count, channels, edge, plane), bf16),
            pltpu.VMEM((count, VALUES * edge, plane), bf16),
            pltpu.SemaphoreType.DMA((count + 3,)),
        ],
        name="decode_bricks",
    )(send_list, density_weight, decode_weight, bricks)


def hat(position, line):
    return jnp.maximum(1.0 - jnp.abs(position - line), 0.0)


def sum_rows(parts):
    row = lax.broadcasted_iota(jnp.int32, parts[0].shape, 0)
    halves = []
    for j in range(4):
        low, high = parts[j], parts[j + 4]
        kept = jnp.where(row < 4, low, high)
        moved = jnp.where(row < 4, high, low)
        both = kept + pltpu.roll(moved, 4, 0)
        both = both + pltpu.roll(both, 1 if j & 1 else 7, 0)
        both = both + pltpu.roll(both, 2 if j & 2 else 6, 0)
        halves.append(both)
    odd = (row & 1) == 1
    pair0 = jnp.where(odd, halves[1], halves[0])
    pair1 = jnp.where(odd, halves[3], halves[2])
    return jnp.where((row & 2) == 2, pair1, pair0)


def sample_run(r, tiles, slot_ref, planes_ref, voxel_ref, frac_ref, column_ref, sampled, shaded, base):
    blocks, samples = voxel_ref.shape[1:]
    capacity = planes_ref.shape[0]
    edge = planes_ref.shape[1] // VALUES
    rays = samples // SPR
    run = blocks // tiles
    batch = 8
    bits = edge.bit_length() - 1
    line = lax.broadcasted_iota(jnp.int32, (edge, samples), 0).astype(f32)
    start = lax.rem(lax.axis_index("tile") + (tiles - r), tiles) * run

    def one_batch(step, carry):
        first = pl.multiple_of(start + step * batch, batch)
        voxel = voxel_ref[0, pl.ds(first, batch), :]
        cells = (voxel >> 2 * bits, (voxel >> bits) & (edge - 1), voxel & (edge - 1))
        at_x, at_y, at_z = [
            cell.astype(f32) + frac_ref[0, axis, pl.ds(first, batch), :] for axis, cell in enumerate(cells)
        ]
        parts = []
        for j in range(batch):
            weight_x = hat(at_x[j : j + 1], line)
            weight_y = hat(at_y[j : j + 1], line)
            weight_z = hat(at_z[j : j + 1], line)
            plane_weights = (
                (weight_y[:, None, :] * weight_z[None, :, :]).reshape(edge * edge, samples).astype(bf16)
            )
            slot = lax.rem(slot_ref[0, first + j], capacity)
            sums = jnp.dot(planes_ref[slot], plane_weights, preferred_element_type=f32)
            sums = sums.reshape(VALUES, edge // 8, 8, samples)
            parts.append(jnp.sum(sums * weight_x.reshape(1, edge // 8, 8, samples), axis=1))
        place = pl.multiple_of(step * batch, batch)
        for k in range(VALUES):
            sampled[k, pl.ds(place, batch), :] = sum_rows([part[k] for part in parts])
        return carry

    lax.fori_loop(0, run // batch, one_batch, 0, unroll=2)
    quarter = lax.broadcasted_iota(jnp.int32, (run, samples), 1) // rays
    rows = pl.ds(pl.multiple_of(start if base is None else base, run), run)
    logit = sampled[0]
    depth = step_length * (jnp.maximum(logit, 0.0) + jnp.log1p(jnp.exp(-jnp.abs(logit))))
    before = jnp.zeros_like(depth)
    total = depth
    for d in range(1, SPR):
        moved = pltpu.roll(depth, d * rays, 1)
        before = before + jnp.where(quarter >= d, moved, 0.0)
        total = total + moved
    weight = jnp.exp(-before) * (1.0 - jnp.exp(-depth))
    placed = quarter == (column_ref[pl.ds(pl.multiple_of(start, run), run), :] & (SPR - 1))
    for k in range(VALUES - 1):
        value = weight * sampled[k + 1]
        value = value + pltpu.roll(value, 2 * rays, 1)
        value = value + pltpu.roll(value, rays, 1)
        shaded[k, rows, :] = jnp.where(placed, value, 0.0).astype(bf16)
    shaded[VALUES - 1, rows, :] = jnp.where(placed, total, 0.0).astype(bf16)


def early_kernel(turns, tiles, slot_ref, voxel_ref, frac_ref, column_ref, *refs):
    planes, (out_ref, sampled) = refs[: len(turns)], refs[len(turns) :]
    run = voxel_ref.shape[1] // tiles
    for i, r in enumerate(turns):
        sample_run(
            r, tiles, slot_ref, planes[i], voxel_ref, frac_ref, column_ref, sampled, out_ref, i * run
        )


def sample_early(turns, tiles, blocks_in, planes):
    blocks, samples = blocks_in[1].shape[1:]
    run = blocks // tiles
    return pl.pallas_call(
        functools.partial(early_kernel, turns, tiles),
        out_shape=jax.ShapeDtypeStruct((VALUES, len(turns) * run, samples), bf16),
        in_specs=[whole(pltpu.SMEM)] + [whole(pltpu.VMEM)] * (3 + len(turns)),
        out_specs=whole(pltpu.VMEM),
        scratch_shapes=[pltpu.VMEM((VALUES, run, samples), f32)],
        compiler_params=pltpu.CompilerParams(vmem_limit_bytes=8 << 20),
        name="sample_early",
    )(*blocks_in, *planes)


def last_kernel(turns, tiles, slot_ref, voxel_ref, frac_ref, column_ref, group_ref, *refs):
    early = refs[: len(turns) - 1]
    planes_ref, out_ref, sampled, shaded = refs[len(turns) - 1 :]
    blocks, samples = voxel_ref.shape[1:]
    run = blocks // tiles
    for done, ref in zip(turns, early):
        for i, r in enumerate(done):
            start = lax.rem(lax.axis_index("tile") + (tiles - r), tiles) * run
            shaded[:, pl.ds(pl.multiple_of(start, run), run), :] = ref[:, i * run : (i + 1) * run, :]
    sample_run(
        turns[-1][0], tiles, slot_ref, planes_ref, voxel_ref, frac_ref, column_ref, sampled, shaded, None
    )
    rows = out_ref.shape[0]
    row = lax.broadcasted_iota(jnp.int32, (rows, blocks), 0)
    owned = (group_ref[...] >> 2) == (row >> 2)
    chosen = [
        (owned & ((row & (VALUES - 1)) == k)).astype(f32).astype(bf16) for k in range(VALUES)
    ]
    placed = jnp.dot(
        jnp.concatenate(chosen, axis=1),
        shaded[...].reshape(VALUES * blocks, samples),
        preferred_element_type=f32,
    )
    out_ref[...] = placed.astype(bf16)


def sample_last(turns, tiles, blocks_in, group, early, planes):
    blocks, samples = blocks_in[1].shape[1:]
    run = blocks // tiles
    return pl.pallas_call(
        functools.partial(last_kernel, turns, tiles),
        out_shape=jax.ShapeDtypeStruct((GROUPS // SPR * VALUES, samples), bf16),
        in_specs=[whole(pltpu.SMEM)] + [whole(pltpu.VMEM)] * (5 + len(early)),
        out_specs=whole(pltpu.VMEM),
        scratch_shapes=[
            pltpu.VMEM((VALUES, run, samples), f32),
            pltpu.VMEM((VALUES, blocks, samples), bf16),
        ],
        compiler_params=pltpu.CompilerParams(vmem_limit_bytes=8 << 20),
        name="sample_last",
    )(*blocks_in, group, *early, planes)


def composite_kernel(got_ref, background_ref, decode_ref, target_ref, colour_ref, loss_ref):
    rows, rays = got_ref.shape
    got = got_ref[...]
    here = lax.broadcasted_iota(jnp.int32, (rows, rows), 0) // VALUES
    there = lax.broadcasted_iota(jnp.int32, (rows, rows), 1)
    nearer = (there // VALUES < here) & (there % VALUES == VALUES - 1)
    depth = jnp.dot(nearer.astype(f32).astype(bf16), got, preferred_element_type=f32)
    is_depth = lax.broadcasted_iota(jnp.int32, (rows, rays), 0) % VALUES == VALUES - 1
    terms = got.astype(f32) * jnp.where(is_depth, 1.0, jnp.exp(-depth))
    total = jnp.sum(terms.reshape(rows // 8, 8, rays), axis=0)
    total = total + pltpu.roll(total, VALUES, 0)
    behind = jnp.sum(decode_ref[...] * background_ref[...], axis=1, keepdims=True)
    logits = total[0:3] + jnp.exp(-total[3:4]) * behind
    colour = jax.nn.sigmoid(logits)
    difference = colour - target_ref[:, 0, :]
    colour_ref[:, 0, :] = colour
    loss_ref[...] = jnp.sum(difference * difference, axis=0, keepdims=True)


def composite(got, background, decode_weight, target):
    rays = got.shape[1]
    return pl.pallas_call(
        composite_kernel,
        out_shape=(
            jax.ShapeDtypeStruct((3, 1, rays), f32),
            jax.ShapeDtypeStruct((1, rays), f32),
        ),
        in_specs=[whole(pltpu.VMEM)] * 4,
        out_specs=(whole(pltpu.VMEM), whole(pltpu.VMEM)),
        compiler_params=pltpu.CompilerParams(vmem_limit_bytes=8 << 20),
        name="composite",
    )(got, background.reshape(1, -1), decode_weight, target)


def on_device(
    bricks,
    send_list,
    sample_voxel,
    sample_frac,
    block_slot,
    block_group,
    density_weight,
    background,
    decode_weight,
    target,
):
    slab_count = lax.axis_size("slab")
    tiles = lax.axis_size("tile")
    blocks = sample_voxel.shape[1]
    planes = list(decode_bricks(send_list, density_weight, decode_weight, bricks))
    for r in (2, 1, 3):
        planes[r] = lax.ppermute(planes[r], "tile", [(i, (i + r) % tiles) for i in range(tiles)])
    blocks_in = (
        block_slot,
        sample_voxel,
        sample_frac.transpose(0, 2, 1, 3),
        block_group.reshape(blocks, 1),
    )
    turns = ((0,), (1, 3), (2,))
    early = [
        sample_early(turn, tiles, blocks_in, [planes[r] for r in turn]) for turn in turns[:-1]
    ]
    placed = sample_last(turns, tiles, blocks_in, block_group, early, planes[turns[-1][0]])
    placed = placed.reshape(slab_count, VALUES, placed.shape[1])
    got = lax.all_to_all(placed, "slab", split_axis=0, concat_axis=0, tiled=True)
    return composite(got.reshape(-1, got.shape[2]), background, decode_weight, target)


def solution(mesh):
    in_specs = (
        P("slab", "tile", None, None, None),
        P("slab", "tile", None),
        P("slab", "tile", None),
        P("slab", "tile", None, None),
        P("slab", "tile"),
        P("slab", "tile"),
        P(),
        P(),
        P(),
        P(None, "tile", "slab"),
    )
    out_specs = (P(None, "tile", "slab"), P("tile", "slab"))
    return jax.shard_map(
        on_device, mesh=mesh, in_specs=in_specs, out_specs=out_specs, check_vma=False
    )
```

time: 51.3 us -> 40.5 us (0.79)
  waiting for transfers between devices: 5.41 us -> 0.01 us
  local copies, waits for them, and re-layouts: 3.76 us -> 0.97 us
  Pallas kernels: 13 us -> 10.8 us
  blocking collectives: 23.1 us -> 22.5 us
    all_to_all x1 -> x0, waiting for transfers between devices: 5.41 us -> none  [on_device(): lax.all_to_all(planes, 'tile', split_axis=0, concat_axis=0, tiled=True)]
    ppermute x0 -> x3, starting transfers between devices: none -> 5.28 us  [on_device(): lax.ppermute(planes[r], 'tile', [(i, (i + r) % tiles) for i in range(tile...]
    all_to_all x1 -> x0, starting transfers between devices: 5.01 us -> none  [on_device(): lax.all_to_all(planes, 'tile', split_axis=0, concat_axis=0, tiled=True)]
    unnamed x22 -> x16, local copies, waits for them, and re-layouts: 3.64 us -> 0.86 us
    pallas_call x2 -> x4, Pallas kernels: 12.2 us -> 9.98 us  [the longest x2 4.65 us: sample_early(): pl.pallas_call(functools.partial(early_kernel, turns, tiles), out_shape=j...]
    all_to_all x1, blocking collectives: 23.1 us -> 22.5 us  [on_device(): lax.all_to_all(placed, 'slab', split_axis=0, concat_axis=0, tiled=True)]
  transfers between devices with their start and end apart: 1 -> 3, of which waited for: 1 -> 0; matrix products, arithmetic and copies ran while one was open for 0% -> 0% of each run, Pallas kernels for 0% -> 12%
where the time goes in v2:
time: 40.5 us; the launch traced here: 40.4 us
  blocking collectives  22.5 us (56%)
  Pallas kernels  10.8 us (27%)
  starting transfers between devices  5.28 us (13%)
  local copies, waits for them, and re-layouts  0.97 us (2%)
  between operations  0.78 us (2%)
    all_to_all x1, blocking collectives, on_device(): lax.all_to_all(placed, 'slab', split_axis=0, concat_axis=0, tiled=True)  22.5 us
    ppermute x3, starting transfers between devices, on_device(): lax.ppermute(planes[r], 'tile', [(i, (i + r) % tiles) for i in range(tile...  5.28 us
    pallas_call x2, Pallas kernels, sample_early(): pl.pallas_call(functools.partial(early_kernel, turns, tiles), out_shape=j...  4.65 us
    pallas_call x1, Pallas kernels, decode_bricks(): pl.pallas_call(decode_kernel, out_shape=(jax.ShapeDtypeStruct((capacity,...  3.36 us
    pallas_call x1, Pallas kernels, sample_last(): pl.pallas_call(functools.partial(last_kernel, turns, tiles), out_shape=ja...  1.97 us
    unnamed x16, local copies, waits for them, and re-layouts  0.86 us
  transfers between devices with their start and end apart: 3, of which 0 were waited for; matrix products, arithmetic and copies ran while one was open for 0% of the time, Pallas kernels for 12%

profile of v2, /device:TPU:1, one launch (start us, length us, event | category | flops | bytes accessed | tf_op | source)
XLA Modules:
  0.0 40.4 jit_solution(15762238404111361512)
XLA Ops:
  0.6 0.0 copy-start.3
  0.6 0.0 copy-start.5
  0.7 0.0 copy-start.4
  0.7 0.0 copy-start.1
  0.7 0.0 copy-start
  0.7 0.0 copy-start.6
  0.7 0.0 copy-start.7
  0.7 3.4 %decode_bricks.1 = (bf16[2,64,256]{2,1,0:T(8,128)(2,1)}, bf16[2,64,256]{2,1,0:T(8,128)(2,1)}, bf16[2,64,256]{2,1,0:T(8,128)(2,1)}, bf16[2,64,256]{2,1,0:T(8,128)(2,1)}) custom-call(s32[1,2,4]{2,1,0:T(2,128)} %bitcast.13, f32[32]{0:T(128)} %density_ref.1, f32[3,32]{1,0:T(4,128)} %decode_ref.3, bf16[1,8,32,16,256]{4,3,2,1,0:T(8,128)(2,1)} %bricks_ref.1), custom_call_target="tpu_custom_call" | custom-call | tf_op jit(solution)/shard_map/decode_bricks/pallas_call | solution.py:67
  4.1 2.2 %collective-permute-start = (bf16[2,64,256]{2,1,0:T(8,128)(2,1)}, bf16[2,64,256]{2,1,0:T(8,128)(2,1)S(1)}, u32[]{:S(2)}, u32[]{:S(2)}) collective-permute-start(bf16[2,64,256]{2,1,0:T(8,128)(2,1)} %get-tuple-element.7), channel_id=1, source_target_pairs={{0,1},{1,2},{2,3},{3,0},{4,5},{5,6},{6,7},{7,4},{8,9},{9,10},{10,1... | collective-permute-start | bytes 196616 | tf_op jit(solution)/shard_map/ppermute | solution.py:278
  6.3 1.5 %collective-permute-start.1 = (bf16[2,64,256]{2,1,0:T(8,128)(2,1)}, bf16[2,64,256]{2,1,0:T(8,128)(2,1)S(1)}, u32[]{:S(2)}, u32[]{:S(2)}) collective-permute-start(bf16[2,64,256]{2,1,0:T(8,128)(2,1)} %get-tuple-element.8), channel_id=1, source_target_pairs={{0,3},{1,0},{2,1},{3,2},{4,7},{5,4},{6,5},{7,6},{8,11},{9,8},{10,9... | collective-permute-start | bytes 196616 | tf_op jit(solution)/shard_map/ppermute | solution.py:278
  7.8 1.6 %collective-permute-start.2 = (bf16[2,64,256]{2,1,0:T(8,128)(2,1)}, bf16[2,64,256]{2,1,0:T(8,128)(2,1)S(1)}, u32[]{:S(2)}, u32[]{:S(2)}) collective-permute-start(bf16[2,64,256]{2,1,0:T(8,128)(2,1)} %get-tuple-element.9), channel_id=1, source_target_pairs={{0,2},{1,3},{2,0},{3,1},{4,6},{5,7},{6,4},{7,5},{8,10},{9,11},{10,... | collective-permute-start | bytes 196616 | tf_op jit(solution)/shard_map/ppermute | solution.py:278
  9.3 0.0 copy-done.5
  9.4 0.1 copy.14.column_ref
  9.5 0.0 copy-done.4
  9.5 0.0 copy-done.1
  9.5 0.0 copy-done
  9.5 0.0 copy-start.2
  9.5 0.8 %copy-done.2 = bf16[2,64,256]{2,1,0:T(8,128)(2,1)S(1)} copy-done((bf16[2,64,256]{2,1,0:T(8,128)(2,1)S(1)}, bf16[2,64,256]{2,1,0:T(8,128)(2,1)}, u32[]{:S(2)}) %copy-start.2) | copy-done | bytes 65560
  10.3 1.7 %sample_early.2.refs_0_ = bf16[4,32,128]{2,1,0:T(8,128)(2,1)S(1)} custom-call(s32[1,128]{1,0:T(1,128)S(1)} %copy-done.4, s32[1,128,128]{2,1,0:T(8,128)S(1)} %copy-done.1, f32[1,3,128,128]{3,2,1,0:T(8,128)S(1)} %bitcast.6, s32[128,1]{1,0:T(8,128)S(1)} %copy.14.column_ref, bf16[2,64,256]{2,1,0:T(8,128)(2,1)S(1)} %copy-done.2), custom_call_target="tpu_custom_call" | custom-call | tf_op jit(solution)/shard_map/sample_early/pallas_call | solution.py:173
  12.1 0.0 collective-permute-done.refs_0_
  12.1 0.0 collective-permute-done.1.refs_1_
  12.1 2.9 %sample_early.3.refs_1_ = bf16[4,64,128]{2,1,0:T(8,128)(2,1)S(1)} custom-call(s32[1,128]{1,0:T(1,128)S(1)} %copy-done.4, s32[1,128,128]{2,1,0:T(8,128)S(1)} %copy-done.1, f32[1,3,128,128]{3,2,1,0:T(8,128)S(1)} %bitcast.7, s32[128,1]{1,0:T(8,128)S(1)} %copy.14.column_ref, bf16[2,64,256]{2,1,0:T(8,128)(2,1)S(1)} %collective-permute-done.refs_0_, ...), custom_call_target="tpu_custom_call" | custom-call | tf_op jit(solution)/shard_map/sample_early/pallas_call | solution.py:173
  15.0 0.0 collective-permute-done.2.refs_2_
  15.0 2.0 %sample_last.1 = bf16[256,128]{1,0:T(8,128)(2,1)S(1)} custom-call(s32[1,128]{1,0:T(1,128)S(1)} %copy-done.4, s32[1,128,128]{2,1,0:T(8,128)S(1)} %copy-done.1, f32[1,3,128,128]{3,2,1,0:T(8,128)S(1)} %bitcast.8, s32[128,1]{1,0:T(8,128)S(1)} %copy.14.column_ref, s32[1,128]{1,0:T(1,128)S(1)} %copy-done.5, bf16[4,32,128]{2,1,0:T(8,128)(2,1)S(1)} %sample_early.2.refs_0_, ...), custom_call_target="tpu_custom_call" | custom-call | tf_op jit(solution)/shard_map/sample_last/pallas_call | solution.py:213
  17.0 22.5 %all_to_all.5 = bf16[64,4,128]{2,1,0:T(4,128)(2,1)S(1)} all-to-all(bf16[64,4,128]{2,1,0:T(4,128)(2,1)S(1)} %bitcast.9), channel_id=1, replica_groups=mesh['slab'=64,'tile'=4] {'slab'}, dimensions={0} | all-to-all | bytes 131072 | tf_op jit(solution)/shard_map/all_to_all | solution.py:291
  39.5 0.0 copy-done.3
  39.6 0.0 copy-done.6
  39.6 0.0 copy-done.7
  39.6 0.8 %composite.1 = (f32[3,1,128]{2,1,0:T(1,128)}, f32[1,128]{1,0:T(1,128)}) custom-call(bf16[256,128]{1,0:T(8,128)(2,1)S(1)} %bitcast.10, f32[1,32]{1,0:T(1,128)S(1)} %bitcast.12, f32[3,32]{1,0:T(4,128)S(1)} %copy-done.3, f32[3,1,128]{2,1,0:T(1,128)S(1)} %copy-done.6), custom_call_target="tpu_custom_call" | custom-call | tf_op jit(solution)/shard_map/composite/pallas_call | solution.py:248
Async XLA Ops:
  0.6 38.9 %copy-start.3 = (f32[3,32]{1,0:T(4,128)S(1)}, f32[3,32]{1,0:T(4,128)}, u32[]{:S(2)}) copy-start(f32[3,32]{1,0:T(4,128)} %decode_ref.3) | copy-start | bytes 1156
  0.6 8.7 %copy-start.5 = (s32[1,128]{1,0:T(1,128)S(1)}, s32[1,128]{1,0:T(1,128)}, u32[]{:S(2)}) copy-start(s32[1,128]{1,0:T(1,128)} %group_ref.1) | copy-start | bytes 1540
  0.7 8.8 %copy-start.4 = (s32[1,128]{1,0:T(1,128)S(1)}, s32[1,128]{1,0:T(1,128)}, u32[]{:S(2)}) copy-start(s32[1,128]{1,0:T(1,128)} %slot_ref.5) | copy-start | bytes 1540
  0.7 8.8 %copy-start.1 = (s32[1,128,128]{2,1,0:T(8,128)S(1)}, s32[1,128,128]{2,1,0:T(8,128)}, u32[]{:S(2)}) copy-start(s32[1,128,128]{2,1,0:T(8,128)} %voxel_ref.5) | copy-start | bytes 196612
  0.7 8.8 %copy-start = (f32[1,128,3,128]{3,1,2,0:T(8,128)S(1)}, f32[1,128,3,128]{3,1,2,0:T(8,128)}, u32[]{:S(2)}) copy-start(f32[1,128,3,128]{3,1,2,0:T(8,128)} %param.13) | copy-start | bytes 589828
  0.7 38.9 %copy-start.6 = (f32[3,1,128]{2,1,0:T(1,128)S(1)}, f32[3,1,128]{2,1,0:T(1,128)}, u32[]{:S(2)}) copy-start(f32[3,1,128]{2,1,0:T(1,128)} %target_ref.1) | copy-start | bytes 4612
  0.7 38.9 %copy-start.7 = (f32[32]{0:T(128)S(1)}, f32[32]{0:T(128)}, u32[]{:S(2)}) copy-start(f32[32]{0:T(128)} %param.17) | copy-start | bytes 388
  4.1 8.0 %collective-permute-start = (bf16[2,64,256]{2,1,0:T(8,128)(2,1)}, bf16[2,64,256]{2,1,0:T(8,128)(2,1)S(1)}, u32[]{:S(2)}, u32[]{:S(2)}) collective-permute-start(bf16[2,64,256]{2,1,0:T(8,128)(2,1)} %get-tuple-element.7), channel_id=1, source_target_pairs={{0,1},{1,2},{2,3},{3,0},{4,5},{5,6},{6,7},{7,4},{8,9},{9,10},{10,1... | collective-permute-start | bytes 196616 | tf_op jit(solution)/shard_map/ppermute | solution.py:278
  6.3 5.8 %collective-permute-start.1 = (bf16[2,64,256]{2,1,0:T(8,128)(2,1)}, bf16[2,64,256]{2,1,0:T(8,128)(2,1)S(1)}, u32[]{:S(2)}, u32[]{:S(2)}) collective-permute-start(bf16[2,64,256]{2,1,0:T(8,128)(2,1)} %get-tuple-element.8), channel_id=1, source_target_pairs={{0,3},{1,0},{2,1},{3,2},{4,7},{5,4},{6,5},{7,6},{8,11},{9,8},{10,9... | collective-permute-start | bytes 196616 | tf_op jit(solution)/shard_map/ppermute | solution.py:278
  7.8 7.2 %collective-permute-start.2 = (bf16[2,64,256]{2,1,0:T(8,128)(2,1)}, bf16[2,64,256]{2,1,0:T(8,128)(2,1)S(1)}, u32[]{:S(2)}, u32[]{:S(2)}) collective-permute-start(bf16[2,64,256]{2,1,0:T(8,128)(2,1)} %get-tuple-element.9), channel_id=1, source_target_pairs={{0,2},{1,3},{2,0},{3,1},{4,6},{5,7},{6,4},{7,5},{8,10},{9,11},{10,... | collective-permute-start | bytes 196616 | tf_op jit(solution)/shard_map/ppermute | solution.py:278
  9.5 0.8 %copy-start.2 = (bf16[2,64,256]{2,1,0:T(8,128)(2,1)S(1)}, bf16[2,64,256]{2,1,0:T(8,128)(2,1)}, u32[]{:S(2)}) copy-start(bf16[2,64,256]{2,1,0:T(8,128)(2,1)} %get-tuple-element.6.refs_0_) | copy-start | bytes 196612

commit v3 on v2

--- a/solution.py
+++ b/solution.py
@@ -8,6 +8,7 @@
 from jax.sharding import PartitionSpec as P
 
 SPR = 4
+EDGE = 16
 GROUPS = 256
 VALUES = 4
 
@@ -55,7 +56,7 @@
     lax.fori_loop(0, bricks, one_brick, 0)
     here = lax.axis_index("tile")
     for r in range(tiles):
-        owner = lax.rem(here + r, tiles)
+        owner = jnp.bitwise_xor(here, r)
         for slot in range(capacity):
             outs[r][slot] = decoded[jnp.clip(send[0, slot, owner], 0, bricks - 1)]
 
@@ -77,8 +78,14 @@
             pltpu.VMEM((count, VALUES * edge, plane), bf16),
             pltpu.SemaphoreType.DMA((count + 3,)),
         ],
+        compiler_params=pltpu.CompilerParams(vmem_limit_bytes=8 << 20),
         name="decode_bricks",
-    )(send_list, density_weight, decode_weight, bricks)
+    )(
+        *[
+            pltpu.with_memory_space_constraint(x, pltpu.HBM)
+            for x in (send_list, density_weight, decode_weight, bricks)
+        ]
+    )
 
 
 def hat(position, line):
@@ -102,7 +109,11 @@
     return jnp.where((row & 2) == 2, pair1, pair0)
 
 
-def sample_run(r, tiles, slot_ref, planes_ref, voxel_ref, frac_ref, column_ref, sampled, shaded, base):
+def every_row(ref, plane, row):
+    return ref[plane, pl.ds(row, 8, stride=0), :]
+
+
+def sample_run(r, tiles, slot_ref, planes_ref, voxel_ref, frac_ref, column_ref, sampled, shaded, base, rows_in, weights_y):
     blocks, samples = voxel_ref.shape[1:]
     capacity = planes_ref.shape[0]
     edge = planes_ref.shape[1] // VALUES
@@ -110,34 +121,51 @@
     run = blocks // tiles
     batch = 8
     bits = edge.bit_length() - 1
-    line = lax.broadcasted_iota(jnp.int32, (edge, samples), 0).astype(f32)
-    start = lax.rem(lax.axis_index("tile") + (tiles - r), tiles) * run
+    line = lax.broadcasted_iota(jnp.int32, (8, samples), 0).astype(f32)
+    lines = [line + low for low in range(0, edge, 8)]
+    turn = jnp.bitwise_xor(lax.axis_index("tile"), r)
+    start = turn * run
+    lane = lax.broadcasted_iota(jnp.int32, slot_ref.shape, 1)
+    second = jnp.where(lane // run == turn, lax.rem(slot_ref[...], capacity) << (lane & (run - 1)), 0)
+    second = jnp.sum(second)
 
     def one_batch(step, carry):
         first = pl.multiple_of(start + step * batch, batch)
         voxel = voxel_ref[0, pl.ds(first, batch), :]
         cells = (voxel >> 2 * bits, (voxel >> bits) & (edge - 1), voxel & (edge - 1))
-        at_x, at_y, at_z = [
-            cell.astype(f32) + frac_ref[0, axis, pl.ds(first, batch), :] for axis, cell in enumerate(cells)
-        ]
+        buffer = (step & 1) * batch
+        for axis, cell in enumerate(cells):
+            rows_in[axis, pl.ds(pl.multiple_of(buffer, batch), batch), :] = (
+                cell.astype(f32) + frac_ref[0, axis, pl.ds(first, batch), :]
+            )
         parts = []
         for j in range(batch):
-            weight_x = hat(at_x[j : j + 1], line)
-            weight_y = hat(at_y[j : j + 1], line)
-            weight_z = hat(at_z[j : j + 1], line)
-            plane_weights = (
-                (weight_y[:, None, :] * weight_z[None, :, :]).reshape(edge * edge, samples).astype(bf16)
+            at_x, at_y, at_z = [every_row(rows_in, axis, buffer + j) for axis in range(3)]
+            weight_x, weight_y, weight_z = [
+                [hat(at, low) for low in lines] for at in (at_x, at_y, at_z)
+            ]
+            weights_y[buffer + j, :8, :] = weight_y[0]
+            weights_y[buffer + j, 8:, :] = weight_y[1]
+            plane_weights = []
+            for y in range(edge):
+                row = every_row(weights_y, buffer + j, y)
+                plane_weights += [row * weight for weight in weight_z]
+            plane_weights = jnp.concatenate(plane_weights, axis=0).astype(bf16)
+            slot = (second >> (step * batch + j)) & 1
+            sums = jnp.dot(planes_ref[slot], plane_weights, preferred_element_type=f32)
+            parts.append(
+                [
+                    sums[k * edge : k * edge + 8] * weight_x[0]
+                    + sums[k * edge + 8 : (k + 1) * edge] * weight_x[1]
+                    for k in range(VALUES)
+                ]
             )
-            slot = lax.rem(slot_ref[0, first + j], capacity)
-            sums = jnp.dot(planes_ref[slot], plane_weights, preferred_element_type=f32)
-            sums = sums.reshape(VALUES, edge // 8, 8, samples)
-            parts.append(jnp.sum(sums * weight_x.reshape(1, edge // 8, 8, samples), axis=1))
         place = pl.multiple_of(step * batch, batch)
         for k in range(VALUES):
             sampled[k, pl.ds(place, batch), :] = sum_rows([part[k] for part in parts])
         return carry
 
-    lax.fori_loop(0, run // batch, one_batch, 0, unroll=2)
+    lax.fori_loop(0, run // batch, one_batch, 0, unroll=4)
     quarter = lax.broadcasted_iota(jnp.int32, (run, samples), 1) // rays
     rows = pl.ds(pl.multiple_of(start if base is None else base, run), run)
     logit = sampled[0]
@@ -158,12 +186,16 @@
     shaded[VALUES - 1, rows, :] = jnp.where(placed, total, 0.0).astype(bf16)
 
 
+def weight_scratch(samples):
+    return [pltpu.VMEM((3, 16, samples), f32), pltpu.VMEM((16, EDGE, samples), f32)]
+
+
 def early_kernel(turns, tiles, slot_ref, voxel_ref, frac_ref, column_ref, *refs):
-    planes, (out_ref, sampled) = refs[: len(turns)], refs[len(turns) :]
+    planes, (out_ref, sampled, *weights) = refs[: len(turns)], refs[len(turns) :]
     run = voxel_ref.shape[1] // tiles
     for i, r in enumerate(turns):
         sample_run(
-            r, tiles, slot_ref, planes[i], voxel_ref, frac_ref, column_ref, sampled, out_ref, i * run
+            r, tiles, slot_ref, planes[i], voxel_ref, frac_ref, column_ref, sampled, out_ref, i * run, *weights
         )
 
 
@@ -173,9 +205,9 @@
     return pl.pallas_call(
         functools.partial(early_kernel, turns, tiles),
         out_shape=jax.ShapeDtypeStruct((VALUES, len(turns) * run, samples), bf16),
-        in_specs=[whole(pltpu.SMEM)] + [whole(pltpu.VMEM)] * (3 + len(turns)),
+        in_specs=[whole(pltpu.VMEM)] * (4 + len(turns)),
         out_specs=whole(pltpu.VMEM),
-        scratch_shapes=[pltpu.VMEM((VALUES, run, samples), f32)],
+        scratch_shapes=[pltpu.VMEM((VALUES, run, samples), f32), *weight_scratch(samples)],
         compiler_params=pltpu.CompilerParams(vmem_limit_bytes=8 << 20),
         name="sample_early",
     )(*blocks_in, *planes)
@@ -183,15 +215,15 @@
 
 def last_kernel(turns, tiles, slot_ref, voxel_ref, frac_ref, column_ref, group_ref, *refs):
     early = refs[: len(turns) - 1]
-    planes_ref, out_ref, sampled, shaded = refs[len(turns) - 1 :]
+    planes_ref, out_ref, sampled, shaded, *weights = refs[len(turns) - 1 :]
     blocks, samples = voxel_ref.shape[1:]
     run = blocks // tiles
     for done, ref in zip(turns, early):
         for i, r in enumerate(done):
-            start = lax.rem(lax.axis_index("tile") + (tiles - r), tiles) * run
+            start = jnp.bitwise_xor(lax.axis_index("tile"), r) * run
             shaded[:, pl.ds(pl.multiple_of(start, run), run), :] = ref[:, i * run : (i + 1) * run, :]
     sample_run(
-        turns[-1][0], tiles, slot_ref, planes_ref, voxel_ref, frac_ref, column_ref, sampled, shaded, None
+        turns[-1][0], tiles, slot_ref, planes_ref, voxel_ref, frac_ref, column_ref, sampled, shaded, None, *weights
     )
     rows = out_ref.shape[0]
     row = lax.broadcasted_iota(jnp.int32, (rows, blocks), 0)
@@ -213,11 +245,12 @@
     return pl.pallas_call(
         functools.partial(last_kernel, turns, tiles),
         out_shape=jax.ShapeDtypeStruct((GROUPS // SPR * VALUES, samples), bf16),
-        in_specs=[whole(pltpu.SMEM)] + [whole(pltpu.VMEM)] * (5 + len(early)),
+        in_specs=[whole(pltpu.VMEM)] * (6 + len(early)),
         out_specs=whole(pltpu.VMEM),
         scratch_shapes=[
             pltpu.VMEM((VALUES, run, samples), f32),
             pltpu.VMEM((VALUES, blocks, samples), bf16),
+            *weight_scratch(samples),
         ],
         compiler_params=pltpu.CompilerParams(vmem_limit_bytes=8 << 20),
         name="sample_last",
@@ -274,8 +307,8 @@
     tiles = lax.axis_size("tile")
     blocks = sample_voxel.shape[1]
     planes = list(decode_bricks(send_list, density_weight, decode_weight, bricks))
-    for r in (2, 1, 3):
-        planes[r] = lax.ppermute(planes[r], "tile", [(i, (i + r) % tiles) for i in range(tiles)])
+    for r in range(1, tiles):
+        planes[r] = lax.ppermute(planes[r], "tile", [(i, i ^ r) for i in range(tiles)])
     blocks_in = (
         block_slot,
         sample_voxel,

time: 40.5 us -> 37.6 us (0.928)
  Pallas kernels: 10.8 us -> 7.03 us
  waiting for transfers between devices: 0.01 us -> 1.38 us
  local copies, waits for them, and re-layouts: 0.97 us -> 0.14 us
  blocking collectives: 22.5 us -> 23.3 us
  starting transfers between devices: 5.28 us -> 4.82 us
    pallas_call x2, Pallas kernels: 4.65 us -> 2.47 us  [sample_early(): pl.pallas_call(functools.partial(early_kernel, turns, tiles), out_shape=j...]
    ppermute x3, waiting for transfers between devices: 0.01 us -> 1.38 us  [on_device(): lax.ppermute(planes[r], 'tile', [(i, i ^ r) for i in range(tiles)])]
    pallas_call x1, Pallas kernels: 1.97 us -> 1.13 us  [sample_last(): pl.pallas_call(functools.partial(last_kernel, turns, tiles), out_shape=ja...]
    unnamed x16 -> x14, local copies, waits for them, and re-layouts: 0.86 us -> 0.03 us
    all_to_all x1, blocking collectives: 22.5 us -> 23.3 us  [on_device(): lax.all_to_all(placed, 'slab', split_axis=0, concat_axis=0, tiled=True)]
    pallas_call x1, Pallas kernels: 3.36 us -> 2.64 us  [decode_bricks(): pl.pallas_call(decode_kernel, out_shape=(jax.ShapeDtypeStruct((capacity,...]
    ppermute x3, starting transfers between devices: 5.28 us -> 4.82 us  [on_device(): lax.ppermute(planes[r], 'tile', [(i, i ^ r) for i in range(tiles)])]
  transfers between devices with their start and end apart: 3 -> 3, of which waited for: 0 -> 2; matrix products, arithmetic and copies ran while one was open for 0% -> 0% of each run, Pallas kernels for 12% -> 7%
where the time goes in v3:
time: 37.6 us; the launch traced here: 37.4 us
  blocking collectives  23.3 us (62%)
  Pallas kernels  7.03 us (19%)
  starting transfers between devices  4.82 us (13%)
  waiting for transfers between devices  1.38 us (4%)
  between operations  0.75 us (2%)
    all_to_all x1, blocking collectives, on_device(): lax.all_to_all(placed, 'slab', split_axis=0, concat_axis=0, tiled=True)  23.3 us
    ppermute x3, starting transfers between devices, on_device(): lax.ppermute(planes[r], 'tile', [(i, i ^ r) for i in range(tiles)])  4.82 us
    pallas_call x1, Pallas kernels, decode_bricks(): pl.pallas_call(decode_kernel, out_shape=(jax.ShapeDtypeStruct((capacity,...  2.64 us
    pallas_call x2, Pallas kernels, sample_early(): pl.pallas_call(functools.partial(early_kernel, turns, tiles), out_shape=j...  2.47 us
    ppermute x3, waiting for transfers between devices, on_device(): lax.ppermute(planes[r], 'tile', [(i, i ^ r) for i in range(tiles)])  1.38 us
    pallas_call x1, Pallas kernels, sample_last(): pl.pallas_call(functools.partial(last_kernel, turns, tiles), out_shape=ja...  1.13 us
    pallas_call x1, Pallas kernels, composite(): pl.pallas_call(composite_kernel, out_shape=(jax.ShapeDtypeStruct((3, 1, r...  0.79 us
  transfers between devices with their start and end apart: 3, of which 2 were waited for; matrix products, arithmetic and copies ran while one was open for 0% of the time, Pallas kernels for 7%

profile of v3, /device:TPU:1, one launch (start us, length us, event | category | flops | bytes accessed | tf_op | source)
XLA Modules:
  0.0 37.4 jit_solution(6359202542864135497)
XLA Ops:
  0.6 0.0 copy-start.2
  0.6 0.0 copy-start.4
  0.7 0.0 copy-start.3
  0.7 0.0 copy-start.1
  0.7 0.0 copy-start
  0.7 0.0 copy-start.5
  0.7 0.0 copy-start.6
  0.7 2.6 %decode_bricks.1 = (bf16[2,64,256]{2,1,0:T(8,128)(2,1)S(1)}, bf16[2,64,256]{2,1,0:T(8,128)(2,1)S(1)}, bf16[2,64,256]{2,1,0:T(8,128)(2,1)S(1)}, bf16[2,64,256]{2,1,0:T(8,128)(2,1)S(1)}) custom-call(s32[1,2,4]{2,1,0:T(2,128)} %bitcast.13, f32[32]{0:T(128)} %density_ref.1, f32[3,32]{1,0:T(4,128)} %decode_ref.3, bf16[1,8,32,16,256]{4,3,2,1,0:T(8,128)(2,1)} %bricks_ref.1), custom_call_target="tpu_custom_call" | custom-call | tf_op jit(solution)/shard_map/decode_bricks/pallas_call | solution.py:68
  3.4 2.2 %collective-permute-start = (bf16[2,64,256]{2,1,0:T(8,128)(2,1)S(1)}, bf16[2,64,256]{2,1,0:T(8,128)(2,1)S(1)}, u32[]{:S(2)}, u32[]{:S(2)}) collective-permute-start(bf16[2,64,256]{2,1,0:T(8,128)(2,1)S(1)} %get-tuple-element.7), channel_id=1, source_target_pairs={{0,1},{1,0},{2,3},{3,2},{4,5},{5,4},{6,7},{7,6},{8,9},{9,8},{10,11... | collective-permute-start | bytes 196616 | tf_op jit(solution)/shard_map/ppermute | solution.py:311
  5.6 1.9 %collective-permute-start.1 = (bf16[2,64,256]{2,1,0:T(8,128)(2,1)S(1)}, bf16[2,64,256]{2,1,0:T(8,128)(2,1)S(1)}, u32[]{:S(2)}, u32[]{:S(2)}) collective-permute-start(bf16[2,64,256]{2,1,0:T(8,128)(2,1)S(1)} %get-tuple-element.8), channel_id=1, source_target_pairs={{0,3},{1,2},{2,1},{3,0},{4,7},{5,6},{6,5},{7,4},{8,11},{9,10},{10,... | collective-permute-start | bytes 196616 | tf_op jit(solution)/shard_map/ppermute | solution.py:311
  7.5 0.7 %collective-permute-start.2 = (bf16[2,64,256]{2,1,0:T(8,128)(2,1)S(1)}, bf16[2,64,256]{2,1,0:T(8,128)(2,1)S(1)}, u32[]{:S(2)}, u32[]{:S(2)}) collective-permute-start(bf16[2,64,256]{2,1,0:T(8,128)(2,1)S(1)} %get-tuple-element.9), channel_id=1, source_target_pairs={{0,2},{1,3},{2,0},{3,1},{4,6},{5,7},{6,4},{7,5},{8,10},{9,11},{10,... | collective-permute-start | bytes 196616 | tf_op jit(solution)/shard_map/ppermute | solution.py:311
  8.2 0.0 copy-done.4
  8.2 0.1 copy.14.column_ref
  8.3 0.0 copy-done.3
  8.3 0.0 copy-done.1
  8.3 0.0 copy-done
  8.3 0.9 %sample_early.2.refs_0_ = bf16[4,32,128]{2,1,0:T(8,128)(2,1)S(1)} custom-call(s32[1,128]{1,0:T(1,128)S(1)} %copy-done.3, s32[1,128,128]{2,1,0:T(8,128)S(1)} %copy-done.1, f32[1,3,128,128]{3,2,1,0:T(8,128)S(1)} %bitcast.6, s32[128,1]{1,0:T(8,128)S(1)} %copy.14.column_ref, bf16[2,64,256]{2,1,0:T(8,128)(2,1)S(1)} %get-tuple-element.6.refs_0_), custom_call_target="tpu_custom_call" | custom-call | tf_op jit(solution)/shard_map/sample_early/pallas_call | solution.py:205
  9.2 0.0 collective-permute-done.refs_0_
  9.3 0.6 %collective-permute-done.1.refs_1_ = bf16[2,64,256]{2,1,0:T(8,128)(2,1)S(1)} collective-permute-done((bf16[2,64,256]{2,1,0:T(8,128)(2,1)S(1)}, bf16[2,64,256]{2,1,0:T(8,128)(2,1)S(1)}, u32[]{:S(2)}, u32[]{:S(2)}) %collective-permute-start.1) | collective-permute-done | bytes 65568 | tf_op jit(solution)/shard_map/ppermute | solution.py:311
  9.9 1.5 %sample_early.3.refs_1_ = bf16[4,64,128]{2,1,0:T(8,128)(2,1)S(1)} custom-call(s32[1,128]{1,0:T(1,128)S(1)} %copy-done.3, s32[1,128,128]{2,1,0:T(8,128)S(1)} %copy-done.1, f32[1,3,128,128]{3,2,1,0:T(8,128)S(1)} %bitcast.7, s32[128,1]{1,0:T(8,128)S(1)} %copy.14.column_ref, bf16[2,64,256]{2,1,0:T(8,128)(2,1)S(1)} %collective-permute-done.refs_0_, ...), custom_call_target="tpu_custom_call" | custom-call | tf_op jit(solution)/shard_map/sample_early/pallas_call | solution.py:205
  11.4 0.7 %collective-permute-done.2.refs_2_ = bf16[2,64,256]{2,1,0:T(8,128)(2,1)S(1)} collective-permute-done((bf16[2,64,256]{2,1,0:T(8,128)(2,1)S(1)}, bf16[2,64,256]{2,1,0:T(8,128)(2,1)S(1)}, u32[]{:S(2)}, u32[]{:S(2)}) %collective-permute-start.2) | collective-permute-done | bytes 65568 | tf_op jit(solution)/shard_map/ppermute | solution.py:311
  12.2 1.1 %sample_last.1 = bf16[256,128]{1,0:T(8,128)(2,1)S(1)} custom-call(s32[1,128]{1,0:T(1,128)S(1)} %copy-done.3, s32[1,128,128]{2,1,0:T(8,128)S(1)} %copy-done.1, f32[1,3,128,128]{3,2,1,0:T(8,128)S(1)} %bitcast.8, s32[128,1]{1,0:T(8,128)S(1)} %copy.14.column_ref, s32[1,128]{1,0:T(1,128)S(1)} %copy-done.4, bf16[4,32,128]{2,1,0:T(8,128)(2,1)S(1)} %sample_early.2.refs_0_, ...), custom_call_target="tpu_custom_call" | custom-call | tf_op jit(solution)/shard_map/sample_last/pallas_call | solution.py:245
  13.3 23.3 %all_to_all.5 = bf16[64,4,128]{2,1,0:T(4,128)(2,1)S(1)} all-to-all(bf16[64,4,128]{2,1,0:T(4,128)(2,1)S(1)} %bitcast.9), channel_id=1, replica_groups=mesh['slab'=64,'tile'=4] {'slab'}, dimensions={0} | all-to-all | bytes 131072 | tf_op jit(solution)/shard_map/all_to_all | solution.py:324
  36.6 0.0 copy-done.2
  36.6 0.0 copy-done.5
  36.6 0.0 copy-done.6
  36.6 0.8 %composite.1 = (f32[3,1,128]{2,1,0:T(1,128)}, f32[1,128]{1,0:T(1,128)}) custom-call(bf16[256,128]{1,0:T(8,128)(2,1)S(1)} %bitcast.10, f32[1,32]{1,0:T(1,128)S(1)} %bitcast.12, f32[3,32]{1,0:T(4,128)S(1)} %copy-done.2, f32[3,1,128]{2,1,0:T(1,128)S(1)} %copy-done.5), custom_call_target="tpu_custom_call" | custom-call | tf_op jit(solution)/shard_map/composite/pallas_call | solution.py:281
Async XLA Ops:
  0.6 36.0 %copy-start.2 = (f32[3,32]{1,0:T(4,128)S(1)}, f32[3,32]{1,0:T(4,128)}, u32[]{:S(2)}) copy-start(f32[3,32]{1,0:T(4,128)} %decode_ref.3) | copy-start | bytes 1156
  0.6 7.5 %copy-start.4 = (s32[1,128]{1,0:T(1,128)S(1)}, s32[1,128]{1,0:T(1,128)}, u32[]{:S(2)}) copy-start(s32[1,128]{1,0:T(1,128)} %group_ref.1) | copy-start | bytes 1540
  0.7 7.6 %copy-start.3 = (s32[1,128]{1,0:T(1,128)S(1)}, s32[1,128]{1,0:T(1,128)}, u32[]{:S(2)}) copy-start(s32[1,128]{1,0:T(1,128)} %slot_ref.5) | copy-start | bytes 1540
  0.7 7.6 %copy-start.1 = (s32[1,128,128]{2,1,0:T(8,128)S(1)}, s32[1,128,128]{2,1,0:T(8,128)}, u32[]{:S(2)}) copy-start(s32[1,128,128]{2,1,0:T(8,128)} %voxel_ref.5) | copy-start | bytes 196612
  0.7 7.6 %copy-start = (f32[1,128,3,128]{3,1,2,0:T(8,128)S(1)}, f32[1,128,3,128]{3,1,2,0:T(8,128)}, u32[]{:S(2)}) copy-start(f32[1,128,3,128]{3,1,2,0:T(8,128)} %param.13) | copy-start | bytes 589828
  0.7 36.0 %copy-start.5 = (f32[3,1,128]{2,1,0:T(1,128)S(1)}, f32[3,1,128]{2,1,0:T(1,128)}, u32[]{:S(2)}) copy-start(f32[3,1,128]{2,1,0:T(1,128)} %target_ref.1) | copy-start | bytes 4612
  0.7 36.0 %copy-start.6 = (f32[32]{0:T(128)S(1)}, f32[32]{0:T(128)}, u32[]{:S(2)}) copy-start(f32[32]{0:T(128)} %param.17) | copy-start | bytes 388
  3.4 5.9 %collective-permute-start = (bf16[2,64,256]{2,1,0:T(8,128)(2,1)S(1)}, bf16[2,64,256]{2,1,0:T(8,128)(2,1)S(1)}, u32[]{:S(2)}, u32[]{:S(2)}) collective-permute-start(bf16[2,64,256]{2,1,0:T(8,128)(2,1)S(1)} %get-tuple-element.7), channel_id=1, source_target_pairs={{0,1},{1,0},{2,3},{3,2},{4,5},{5,4},{6,7},{7,6},{8,9},{9,8},{10,11... | collective-permute-start | bytes 196616 | tf_op jit(solution)/shard_map/ppermute | solution.py:311
  5.6 4.3 %collective-permute-start.1 = (bf16[2,64,256]{2,1,0:T(8,128)(2,1)S(1)}, bf16[2,64,256]{2,1,0:T(8,128)(2,1)S(1)}, u32[]{:S(2)}, u32[]{:S(2)}) collective-permute-start(bf16[2,64,256]{2,1,0:T(8,128)(2,1)S(1)} %get-tuple-element.8), channel_id=1, source_target_pairs={{0,3},{1,2},{2,1},{3,0},{4,7},{5,6},{6,5},{7,4},{8,11},{9,10},{10,... | collective-permute-start | bytes 196616 | tf_op jit(solution)/shard_map/ppermute | solution.py:311
  7.5 4.7 %collective-permute-start.2 = (bf16[2,64,256]{2,1,0:T(8,128)(2,1)S(1)}, bf16[2,64,256]{2,1,0:T(8,128)(2,1)S(1)}, u32[]{:S(2)}, u32[]{:S(2)}) collective-permute-start(bf16[2,64,256]{2,1,0:T(8,128)(2,1)S(1)} %get-tuple-element.9), channel_id=1, source_target_pairs={{0,2},{1,3},{2,0},{3,1},{4,6},{5,7},{6,4},{7,5},{8,10},{9,11},{10,... | collective-permute-start | bytes 196616 | tf_op jit(solution)/shard_map/ppermute | solution.py:311

commit v4 on v3

--- a/solution.py
+++ b/solution.py
@@ -22,15 +22,23 @@
 
 
 def decode_kernel(send_ref, density_ref, decode_ref, bricks_ref, *refs):
-    tiles = len(refs) - 6
+    tiles = len(refs) - 9
     outs = refs[:tiles]
-    send, density, decode, buffer, decoded, sems = refs[tiles:]
+    send, density, decode, density_row, decode_rows, buffer, spread, decoded, sems = refs[tiles:]
     capacity = outs[0].shape[0]
     bricks, channels, edge, plane = bricks_ref.shape[1:]
+    columns = channels * edge
+    half = VALUES * edge
     small = [
         pltpu.make_async_copy(source, target, sems.at[bricks + i])
         for i, (source, target) in enumerate(
-            ((send_ref, send), (density_ref, density), (decode_ref, decode))
+            (
+                (density_ref, density_row),
+                (decode_ref, decode_rows),
+                (send_ref, send),
+                (density_ref, density),
+                (decode_ref, decode),
+            )
         )
     ]
     large = [
@@ -42,18 +50,38 @@
     for copy in small:
         copy.wait()
 
-    def one_brick(brick, carry):
-        pltpu.make_async_copy(bricks_ref.at[0, brick], buffer.at[brick], sems.at[brick]).wait()
+    heads = jnp.concatenate([density_row[...], decode_rows[...]], axis=0)
+    coarse = heads.astype(bf16)
+    fine = (heads - coarse.astype(f32)).astype(bf16)
+    repeat = lax.broadcasted_iota(jnp.int32, (channels, columns), 1) // edge == (
+        lax.broadcasted_iota(jnp.int32, (channels, columns), 0)
+    )
+    diagonal = (lax.broadcasted_iota(jnp.int32, (edge, columns), 1) & (edge - 1)) == (
+        lax.broadcasted_iota(jnp.int32, (edge, columns), 0)
+    )
+    for part, term in enumerate((coarse, fine)):
+        wide = jnp.dot(term, repeat.astype(f32).astype(bf16), preferred_element_type=f32)
+        for k in range(VALUES):
+            row = (part * VALUES + k) * edge
+            spread[row : row + edge, :] = jnp.where(diagonal, wide[k : k + 1], 0.0).astype(bf16)
+
+    def one_pair(pair, carry):
+        for brick in (2 * pair, 2 * pair + 1):
+            pltpu.make_async_copy(bricks_ref.at[0, brick], buffer.at[brick], sems.at[brick]).wait()
+        both = jnp.dot(
+            spread[...], buffer[2 * pair].reshape(columns, plane), preferred_element_type=f32
+        )
+        decoded[2 * pair] = (both[:half] + both[half:]).astype(bf16)
         sums = [jnp.zeros((edge, plane), f32) for _ in range(VALUES)]
         for c in range(channels):
-            values = buffer[brick, c].astype(f32)
-            weights = [density[c]] + [decode[k, c] for k in range(VALUES - 1)]
+            values = buffer[2 * pair + 1, c].astype(f32)
+            weights = [density[0, c]] + [decode[k, c] for k in range(VALUES - 1)]
             sums = [total + weight * values for total, weight in zip(sums, weights)]
         for k in range(VALUES):
-            decoded[brick, k * edge : (k + 1) * edge, :] = sums[k].astype(bf16)
+            decoded[2 * pair + 1, k * edge : (k + 1) * edge, :] = sums[k].astype(bf16)
         return carry
 
-    lax.fori_loop(0, bricks, one_brick, 0)
+    lax.fori_loop(0, bricks // 2, one_pair, 0)
     here = lax.axis_index("tile")
     for r in range(tiles):
         owner = jnp.bitwise_xor(here, r)
@@ -65,6 +93,7 @@
     tiles, capacity = send_list.shape[1:]
     send_list = send_list.transpose(0, 2, 1)
     count, channels, edge, plane = bricks.shape[1:]
+    density_weight = density_weight.reshape(1, channels)
     return pl.pallas_call(
         decode_kernel,
         out_shape=(jax.ShapeDtypeStruct((capacity, VALUES * edge, plane), bf16),) * tiles,
@@ -74,9 +103,12 @@
             pltpu.SMEM(send_list.shape, jnp.int32),
             pltpu.SMEM(density_weight.shape, f32),
             pltpu.SMEM(decode_weight.shape, f32),
+            pltpu.VMEM(density_weight.shape, f32),
+            pltpu.VMEM(decode_weight.shape, f32),
             pltpu.VMEM((count, channels, edge, plane), bf16),
+            pltpu.VMEM((2 * VALUES * edge, channels * edge), bf16),
             pltpu.VMEM((count, VALUES * edge, plane), bf16),
-            pltpu.SemaphoreType.DMA((count + 3,)),
+            pltpu.SemaphoreType.DMA((count + 5,)),
         ],
         compiler_params=pltpu.CompilerParams(vmem_limit_bytes=8 << 20),
         name="decode_bricks",

time: 37.6 us -> 37.2 us (0.989)
  no operation moved by 1% of the time
where the time goes in v4:
time: 37.2 us; the launch traced here: 37.1 us
  blocking collectives  23.3 us (63%)
  Pallas kernels  6.72 us (18%)
  starting transfers between devices  4.82 us (13%)
  waiting for transfers between devices  1.37 us (4%)
  between operations  0.74 us (2%)
    all_to_all x1, blocking collectives, on_device(): lax.all_to_all(placed, 'slab', split_axis=0, concat_axis=0, tiled=True)  23.3 us
    ppermute x3, starting transfers between devices, on_device(): lax.ppermute(planes[r], 'tile', [(i, i ^ r) for i in range(tiles)])  4.82 us
    pallas_call x2, Pallas kernels, sample_early(): pl.pallas_call(functools.partial(early_kernel, turns, tiles), out_shape=j...  2.47 us
    pallas_call x1, Pallas kernels, decode_bricks(): pl.pallas_call(decode_kernel, out_shape=(jax.ShapeDtypeStruct((capacity,...  2.32 us
    ppermute x3, waiting for transfers between devices, on_device(): lax.ppermute(planes[r], 'tile', [(i, i ^ r) for i in range(tiles)])  1.37 us
    pallas_call x1, Pallas kernels, sample_last(): pl.pallas_call(functools.partial(last_kernel, turns, tiles), out_shape=ja...  1.15 us
    pallas_call x1, Pallas kernels, composite(): pl.pallas_call(composite_kernel, out_shape=(jax.ShapeDtypeStruct((3, 1, r...  0.79 us
  transfers between devices with their start and end apart: 3, of which 2 were waited for; matrix products, arithmetic and copies ran while one was open for 0% of the time, Pallas kernels for 7%

profile of v4, /device:TPU:1, one launch (start us, length us, event | category | flops | bytes accessed | tf_op | source)
XLA Modules:
  0.0 37.1 jit_solution(2986107776619263216)
XLA Ops:
  0.6 0.0 copy-start.2
  0.6 0.0 copy-start.4
  0.7 0.0 copy-start.3
  0.7 0.0 copy-start.1
  0.7 0.0 copy-start
  0.7 0.0 copy-start.5
  0.7 0.0 copy-start.6
  0.7 2.3 %decode_bricks.1 = (bf16[2,64,256]{2,1,0:T(8,128)(2,1)S(1)}, bf16[2,64,256]{2,1,0:T(8,128)(2,1)S(1)}, bf16[2,64,256]{2,1,0:T(8,128)(2,1)S(1)}, bf16[2,64,256]{2,1,0:T(8,128)(2,1)S(1)}) custom-call(s32[1,2,4]{2,1,0:T(2,128)} %bitcast.14, f32[1,32]{1,0:T(1,128)} %bitcast.15, f32[3,32]{1,0:T(4,128)} %decode_ref.3, bf16[1,8,32,16,256]{4,3,2,1,0:T(8,128)(2,1)} %bricks_ref.1), custom_call_target="tpu_custom_call" | custom-call | tf_op jit(solution)/shard_map/decode_bricks/pallas_call | solution.py:97
  3.0 2.2 %collective-permute-start = (bf16[2,64,256]{2,1,0:T(8,128)(2,1)S(1)}, bf16[2,64,256]{2,1,0:T(8,128)(2,1)S(1)}, u32[]{:S(2)}, u32[]{:S(2)}) collective-permute-start(bf16[2,64,256]{2,1,0:T(8,128)(2,1)S(1)} %get-tuple-element.7), channel_id=1, source_target_pairs={{0,1},{1,0},{2,3},{3,2},{4,5},{5,4},{6,7},{7,6},{8,9},{9,8},{10,11... | collective-permute-start | bytes 196616 | tf_op jit(solution)/shard_map/ppermute | solution.py:343
  5.2 1.9 %collective-permute-start.1 = (bf16[2,64,256]{2,1,0:T(8,128)(2,1)S(1)}, bf16[2,64,256]{2,1,0:T(8,128)(2,1)S(1)}, u32[]{:S(2)}, u32[]{:S(2)}) collective-permute-start(bf16[2,64,256]{2,1,0:T(8,128)(2,1)S(1)} %get-tuple-element.8), channel_id=1, source_target_pairs={{0,3},{1,2},{2,1},{3,0},{4,7},{5,6},{6,5},{7,4},{8,11},{9,10},{10,... | collective-permute-start | bytes 196616 | tf_op jit(solution)/shard_map/ppermute | solution.py:343
  7.1 0.7 %collective-permute-start.2 = (bf16[2,64,256]{2,1,0:T(8,128)(2,1)S(1)}, bf16[2,64,256]{2,1,0:T(8,128)(2,1)S(1)}, u32[]{:S(2)}, u32[]{:S(2)}) collective-permute-start(bf16[2,64,256]{2,1,0:T(8,128)(2,1)S(1)} %get-tuple-element.9), channel_id=1, source_target_pairs={{0,2},{1,3},{2,0},{3,1},{4,6},{5,7},{6,4},{7,5},{8,10},{9,11},{10,... | collective-permute-start | bytes 196616 | tf_op jit(solution)/shard_map/ppermute | solution.py:343
  7.8 0.0 copy-done.4
  7.8 0.1 copy.14.column_ref
  8.0 0.0 copy-done.3
  8.0 0.0 copy-done.1
  8.0 0.0 copy-done
  8.0 0.9 %sample_early.2.refs_0_ = bf16[4,32,128]{2,1,0:T(8,128)(2,1)S(1)} custom-call(s32[1,128]{1,0:T(1,128)S(1)} %copy-done.3, s32[1,128,128]{2,1,0:T(8,128)S(1)} %copy-done.1, f32[1,3,128,128]{3,2,1,0:T(8,128)S(1)} %bitcast.7, s32[128,1]{1,0:T(8,128)S(1)} %copy.14.column_ref, bf16[2,64,256]{2,1,0:T(8,128)(2,1)S(1)} %get-tuple-element.6.refs_0_), custom_call_target="tpu_custom_call" | custom-call | tf_op jit(solution)/shard_map/sample_early/pallas_call | solution.py:237
  8.9 0.0 collective-permute-done.refs_0_
  8.9 0.6 %collective-permute-done.1.refs_1_ = bf16[2,64,256]{2,1,0:T(8,128)(2,1)S(1)} collective-permute-done((bf16[2,64,256]{2,1,0:T(8,128)(2,1)S(1)}, bf16[2,64,256]{2,1,0:T(8,128)(2,1)S(1)}, u32[]{:S(2)}, u32[]{:S(2)}) %collective-permute-start.1) | collective-permute-done | bytes 65568 | tf_op jit(solution)/shard_map/ppermute | solution.py:343
  9.6 1.6 %sample_early.3.refs_1_ = bf16[4,64,128]{2,1,0:T(8,128)(2,1)S(1)} custom-call(s32[1,128]{1,0:T(1,128)S(1)} %copy-done.3, s32[1,128,128]{2,1,0:T(8,128)S(1)} %copy-done.1, f32[1,3,128,128]{3,2,1,0:T(8,128)S(1)} %bitcast.8, s32[128,1]{1,0:T(8,128)S(1)} %copy.14.column_ref, bf16[2,64,256]{2,1,0:T(8,128)(2,1)S(1)} %collective-permute-done.refs_0_, ...), custom_call_target="tpu_custom_call" | custom-call | tf_op jit(solution)/shard_map/sample_early/pallas_call | solution.py:237
  11.1 0.7 %collective-permute-done.2.refs_2_ = bf16[2,64,256]{2,1,0:T(8,128)(2,1)S(1)} collective-permute-done((bf16[2,64,256]{2,1,0:T(8,128)(2,1)S(1)}, bf16[2,64,256]{2,1,0:T(8,128)(2,1)S(1)}, u32[]{:S(2)}, u32[]{:S(2)}) %collective-permute-start.2) | collective-permute-done | bytes 65568 | tf_op jit(solution)/shard_map/ppermute | solution.py:343
  11.8 1.1 %sample_last.1 = bf16[256,128]{1,0:T(8,128)(2,1)S(1)} custom-call(s32[1,128]{1,0:T(1,128)S(1)} %copy-done.3, s32[1,128,128]{2,1,0:T(8,128)S(1)} %copy-done.1, f32[1,3,128,128]{3,2,1,0:T(8,128)S(1)} %bitcast.9, s32[128,1]{1,0:T(8,128)S(1)} %copy.14.column_ref, s32[1,128]{1,0:T(1,128)S(1)} %copy-done.4, bf16[4,32,128]{2,1,0:T(8,128)(2,1)S(1)} %sample_early.2.refs_0_, ...), custom_call_target="tpu_custom_call" | custom-call | tf_op jit(solution)/shard_map/sample_last/pallas_call | solution.py:277
  13.0 23.3 %all_to_all.5 = bf16[64,4,128]{2,1,0:T(4,128)(2,1)S(1)} all-to-all(bf16[64,4,128]{2,1,0:T(4,128)(2,1)S(1)} %bitcast.10), channel_id=1, replica_groups=mesh['slab'=64,'tile'=4] {'slab'}, dimensions={0} | all-to-all | bytes 131072 | tf_op jit(solution)/shard_map/all_to_all | solution.py:356
  36.3 0.0 copy-done.2
  36.3 0.0 copy-done.5
  36.3 0.0 copy-done.6
  36.3 0.8 %composite.1 = (f32[3,1,128]{2,1,0:T(1,128)}, f32[1,128]{1,0:T(1,128)}) custom-call(bf16[256,128]{1,0:T(8,128)(2,1)S(1)} %bitcast.11, f32[1,32]{1,0:T(1,128)S(1)} %bitcast.13, f32[3,32]{1,0:T(4,128)S(1)} %copy-done.2, f32[3,1,128]{2,1,0:T(1,128)S(1)} %copy-done.5), custom_call_target="tpu_custom_call" | custom-call | tf_op jit(solution)/shard_map/composite/pallas_call | solution.py:313
Async XLA Ops:
  0.6 35.7 %copy-start.2 = (f32[3,32]{1,0:T(4,128)S(1)}, f32[3,32]{1,0:T(4,128)}, u32[]{:S(2)}) copy-start(f32[3,32]{1,0:T(4,128)} %decode_ref.3) | copy-start | bytes 1156
  0.6 7.2 %copy-start.4 = (s32[1,128]{1,0:T(1,128)S(1)}, s32[1,128]{1,0:T(1,128)}, u32[]{:S(2)}) copy-start(s32[1,128]{1,0:T(1,128)} %group_ref.1) | copy-start | bytes 1540
  0.7 7.3 %copy-start.3 = (s32[1,128]{1,0:T(1,128)S(1)}, s32[1,128]{1,0:T(1,128)}, u32[]{:S(2)}) copy-start(s32[1,128]{1,0:T(1,128)} %slot_ref.5) | copy-start | bytes 1540
  0.7 7.3 %copy-start.1 = (s32[1,128,128]{2,1,0:T(8,128)S(1)}, s32[1,128,128]{2,1,0:T(8,128)}, u32[]{:S(2)}) copy-start(s32[1,128,128]{2,1,0:T(8,128)} %voxel_ref.5) | copy-start | bytes 196612
  0.7 7.3 %copy-start = (f32[1,128,3,128]{3,1,2,0:T(8,128)S(1)}, f32[1,128,3,128]{3,1,2,0:T(8,128)}, u32[]{:S(2)}) copy-start(f32[1,128,3,128]{3,1,2,0:T(8,128)} %param.13) | copy-start | bytes 589828
  0.7 35.6 %copy-start.5 = (f32[3,1,128]{2,1,0:T(1,128)S(1)}, f32[3,1,128]{2,1,0:T(1,128)}, u32[]{:S(2)}) copy-start(f32[3,1,128]{2,1,0:T(1,128)} %target_ref.1) | copy-start | bytes 4612
  0.7 35.6 %copy-start.6 = (f32[32]{0:T(128)S(1)}, f32[32]{0:T(128)}, u32[]{:S(2)}) copy-start(f32[32]{0:T(128)} %param.17) | copy-start | bytes 388
  3.0 5.9 %collective-permute-start = (bf16[2,64,256]{2,1,0:T(8,128)(2,1)S(1)}, bf16[2,64,256]{2,1,0:T(8,128)(2,1)S(1)}, u32[]{:S(2)}, u32[]{:S(2)}) collective-permute-start(bf16[2,64,256]{2,1,0:T(8,128)(2,1)S(1)} %get-tuple-element.7), channel_id=1, source_target_pairs={{0,1},{1,0},{2,3},{3,2},{4,5},{5,4},{6,7},{7,6},{8,9},{9,8},{10,11... | collective-permute-start | bytes 196616 | tf_op jit(solution)/shard_map/ppermute | solution.py:343
  5.2 4.3 %collective-permute-start.1 = (bf16[2,64,256]{2,1,0:T(8,128)(2,1)S(1)}, bf16[2,64,256]{2,1,0:T(8,128)(2,1)S(1)}, u32[]{:S(2)}, u32[]{:S(2)}) collective-permute-start(bf16[2,64,256]{2,1,0:T(8,128)(2,1)S(1)} %get-tuple-element.8), channel_id=1, source_target_pairs={{0,3},{1,2},{2,1},{3,0},{4,7},{5,6},{6,5},{7,4},{8,11},{9,10},{10,... | collective-permute-start | bytes 196616 | tf_op jit(solution)/shard_map/ppermute | solution.py:343
  7.1 4.7 %collective-permute-start.2 = (bf16[2,64,256]{2,1,0:T(8,128)(2,1)S(1)}, bf16[2,64,256]{2,1,0:T(8,128)(2,1)S(1)}, u32[]{:S(2)}, u32[]{:S(2)}) collective-permute-start(bf16[2,64,256]{2,1,0:T(8,128)(2,1)S(1)} %get-tuple-element.9), channel_id=1, source_target_pairs={{0,2},{1,3},{2,0},{3,1},{4,6},{5,7},{6,4},{7,5},{8,10},{9,11},{10,... | collective-permute-start | bytes 196616 | tf_op jit(solution)/shard_map/ppermute | solution.py:343

commit v5 on v4

--- a/solution.py
+++ b/solution.py
@@ -7,8 +7,11 @@
 from jax.experimental.pallas import tpu as pltpu
 from jax.sharding import PartitionSpec as P
 
+
 SPR = 4
 EDGE = 16
+ORDER = (3, 1, 2)
+TURNS = ((0, 3), (1,), (2,))
 GROUPS = 256
 VALUES = 4
 
@@ -223,7 +226,7 @@
 
 
 def early_kernel(turns, tiles, slot_ref, voxel_ref, frac_ref, column_ref, *refs):
-    planes, (out_ref, sampled, *weights) = refs[: len(turns)], refs[len(turns) :]
+    planes, (out_ref, sampled, *weights) = refs[: len(turns)], refs[-4:]
     run = voxel_ref.shape[1] // tiles
     for i, r in enumerate(turns):
         sample_run(
@@ -231,18 +234,18 @@
         )
 
 
-def sample_early(turns, tiles, blocks_in, planes):
+def sample_early(turns, tiles, blocks_in, planes, before):
     blocks, samples = blocks_in[1].shape[1:]
     run = blocks // tiles
     return pl.pallas_call(
         functools.partial(early_kernel, turns, tiles),
         out_shape=jax.ShapeDtypeStruct((VALUES, len(turns) * run, samples), bf16),
-        in_specs=[whole(pltpu.VMEM)] * (4 + len(turns)),
+        in_specs=[whole(pltpu.VMEM)] * (4 + len(turns)) + [whole(pl.ANY)] * len(before),
         out_specs=whole(pltpu.VMEM),
         scratch_shapes=[pltpu.VMEM((VALUES, run, samples), f32), *weight_scratch(samples)],
         compiler_params=pltpu.CompilerParams(vmem_limit_bytes=8 << 20),
         name="sample_early",
-    )(*blocks_in, *planes)
+    )(*blocks_in, *planes, *before)
 
 
 def last_kernel(turns, tiles, slot_ref, voxel_ref, frac_ref, column_ref, group_ref, *refs):
@@ -323,7 +326,7 @@
     )(got, background.reshape(1, -1), decode_weight, target)
 
 
-def on_device(
+def stages(
     bricks,
     send_list,
     sample_voxel,
@@ -339,7 +342,7 @@
     tiles = lax.axis_size("tile")
     blocks = sample_voxel.shape[1]
     planes = list(decode_bricks(send_list, density_weight, decode_weight, bricks))
-    for r in range(1, tiles):
+    for r in ORDER:
         planes[r] = lax.ppermute(planes[r], "tile", [(i, i ^ r) for i in range(tiles)])
     blocks_in = (
         block_slot,
@@ -347,10 +350,10 @@
         sample_frac.transpose(0, 2, 1, 3),
         block_group.reshape(blocks, 1),
     )
-    turns = ((0,), (1, 3), (2,))
-    early = [
-        sample_early(turn, tiles, blocks_in, [planes[r] for r in turn]) for turn in turns[:-1]
-    ]
+    turns = TURNS
+    early = []
+    for turn in turns[:-1]:
+        early.append(sample_early(turn, tiles, blocks_in, [planes[r] for r in turn], early[-1:]))
     placed = sample_last(turns, tiles, blocks_in, block_group, early, planes[turns[-1][0]])
     placed = placed.reshape(slab_count, VALUES, placed.shape[1])
     got = lax.all_to_all(placed, "slab", split_axis=0, concat_axis=0, tiled=True)
@@ -371,6 +374,4 @@
         P(None, "tile", "slab"),
     )
     out_specs = (P(None, "tile", "slab"), P("tile", "slab"))
-    return jax.shard_map(
-        on_device, mesh=mesh, in_specs=in_specs, out_specs=out_specs, check_vma=False
-    )
+    return jax.shard_map(stages, mesh=mesh, in_specs=in_specs, out_specs=out_specs, check_vma=False)

time: 37.2 us -> 36.7 us (0.987)
  waiting for transfers between devices: 1.37 us -> 0.83 us
    ppermute x3, waiting for transfers between devices: 1.37 us -> 0.83 us  [stages(): lax.ppermute(planes[r], 'tile', [(i, i ^ r) for i in range(tiles)])]
where the time goes in v5:
time: 36.7 us; the launch traced here: 36.5 us
  blocking collectives  23.2 us (63%)
  Pallas kernels  6.75 us (18%)
  starting transfers between devices  4.92 us (13%)
  waiting for transfers between devices  0.83 us (2%)
  between operations  0.72 us (2%)
    all_to_all x1, blocking collectives, stages(): lax.all_to_all(placed, 'slab', split_axis=0, concat_axis=0, tiled=True)  23.2 us
    ppermute x3, starting transfers between devices, stages(): lax.ppermute(planes[r], 'tile', [(i, i ^ r) for i in range(tiles)])  4.92 us
    pallas_call x2, Pallas kernels, sample_early(): pl.pallas_call(functools.partial(early_kernel, turns, tiles), out_shape=j...  2.48 us
    pallas_call x1, Pallas kernels, decode_bricks(): pl.pallas_call(decode_kernel, out_shape=(jax.ShapeDtypeStruct((capacity,...  2.34 us
    pallas_call x1, Pallas kernels, sample_last(): pl.pallas_call(functools.partial(last_kernel, turns, tiles), out_shape=ja...  1.13 us
    ppermute x3, waiting for transfers between devices, stages(): lax.ppermute(planes[r], 'tile', [(i, i ^ r) for i in range(tiles)])  0.83 us
    pallas_call x1, Pallas kernels, composite(): pl.pallas_call(composite_kernel, out_shape=(jax.ShapeDtypeStruct((3, 1, r...  0.79 us
  transfers between devices with their start and end apart: 3, of which 2 were waited for; matrix products, arithmetic and copies ran while one was open for 0% of the time, Pallas kernels for 7%

profile of v5, /device:TPU:1, one launch (start us, length us, event | category | flops | bytes accessed | tf_op | source)
XLA Modules:
  0.0 36.5 jit_solution(6527813592245718556)
XLA Ops:
  0.6 0.0 copy-start.2
  0.6 0.0 copy-start.4
  0.7 0.0 copy-start
  0.7 0.0 copy-start.1
  0.7 0.0 copy-start.3
  0.7 0.0 copy-start.6
  0.7 0.0 copy-start.5
  0.7 2.3 %decode_bricks.1 = (bf16[2,64,256]{2,1,0:T(8,128)(2,1)S(1)}, bf16[2,64,256]{2,1,0:T(8,128)(2,1)S(1)}, bf16[2,64,256]{2,1,0:T(8,128)(2,1)S(1)}, bf16[2,64,256]{2,1,0:T(8,128)(2,1)S(1)}) custom-call(s32[1,2,4]{2,1,0:T(2,128)} %bitcast.14, f32[1,32]{1,0:T(1,128)} %bitcast.15, f32[3,32]{1,0:T(4,128)} %decode_ref.3, bf16[1,8,32,16,256]{4,3,2,1,0:T(8,128)(2,1)} %bricks_ref.1), custom_call_target="tpu_custom_call" | custom-call | tf_op jit(solution)/shard_map/decode_bricks/pallas_call | solution.py:100
  3.1 3.6 %collective-permute-start = (bf16[2,64,256]{2,1,0:T(8,128)(2,1)S(1)}, bf16[2,64,256]{2,1,0:T(8,128)(2,1)S(1)}, u32[]{:S(2)}, u32[]{:S(2)}) collective-permute-start(bf16[2,64,256]{2,1,0:T(8,128)(2,1)S(1)} %get-tuple-element.7), channel_id=1, source_target_pairs={{0,3},{1,2},{2,1},{3,0},{4,7},{5,6},{6,5},{7,4},{8,11},{9,10},{10,... | collective-permute-start | bytes 196616 | tf_op jit(solution)/shard_map/ppermute | solution.py:346
  6.7 0.0 collective-permute-start.1
  6.7 1.3 %collective-permute-start.2 = (bf16[2,64,256]{2,1,0:T(8,128)(2,1)S(1)}, bf16[2,64,256]{2,1,0:T(8,128)(2,1)S(1)}, u32[]{:S(2)}, u32[]{:S(2)}) collective-permute-start(bf16[2,64,256]{2,1,0:T(8,128)(2,1)S(1)} %get-tuple-element.9), channel_id=1, source_target_pairs={{0,2},{1,3},{2,0},{3,1},{4,6},{5,7},{6,4},{7,5},{8,10},{9,11},{10,... | collective-permute-start | bytes 196616 | tf_op jit(solution)/shard_map/ppermute | solution.py:346
  8.0 0.0 copy-done.4
  8.0 0.1 copy.14.column_ref
  8.1 0.3 collective-permute-done.refs_1_
  8.3 0.0 copy-done
  8.4 0.0 copy-done.1
  8.4 0.0 copy-done.3
  8.4 1.5 %sample_early.2.refs_1_.refs_0_ = bf16[4,64,128]{2,1,0:T(8,128)(2,1)S(1)} custom-call(s32[1,128]{1,0:T(1,128)S(1)} %copy-done.3, s32[1,128,128]{2,1,0:T(8,128)S(1)} %copy-done.1, f32[1,3,128,128]{3,2,1,0:T(8,128)S(1)} %bitcast.7, s32[128,1]{1,0:T(8,128)S(1)} %copy.14.column_ref, bf16[2,64,256]{2,1,0:T(8,128)(2,1)S(1)} %get-tuple-element.6.refs_0_, ...), custom_call_target="tpu_custom_call" | custom-call | tf_op jit(solution)/shard_map/sample_early/pallas_call | solution.py:240
  9.9 0.0 collective-permute-done.1.refs_0_
  9.9 0.9 %sample_early.3.refs_1_ = bf16[4,32,128]{2,1,0:T(8,128)(2,1)S(1)} custom-call(s32[1,128]{1,0:T(1,128)S(1)} %copy-done.3, s32[1,128,128]{2,1,0:T(8,128)S(1)} %copy-done.1, f32[1,3,128,128]{3,2,1,0:T(8,128)S(1)} %bitcast.8, s32[128,1]{1,0:T(8,128)S(1)} %copy.14.column_ref, bf16[2,64,256]{2,1,0:T(8,128)(2,1)S(1)} %collective-permute-done.1.refs_0_, ...), custom_call_target="tpu_custom_call" | custom-call | tf_op jit(solution)/shard_map/sample_early/pallas_call | solution.py:240
  10.9 0.6 %collective-permute-done.2.refs_2_ = bf16[2,64,256]{2,1,0:T(8,128)(2,1)S(1)} collective-permute-done((bf16[2,64,256]{2,1,0:T(8,128)(2,1)S(1)}, bf16[2,64,256]{2,1,0:T(8,128)(2,1)S(1)}, u32[]{:S(2)}, u32[]{:S(2)}) %collective-permute-start.2) | collective-permute-done | bytes 65568 | tf_op jit(solution)/shard_map/ppermute | solution.py:346
  11.4 1.1 %sample_last.1 = bf16[256,128]{1,0:T(8,128)(2,1)S(1)} custom-call(s32[1,128]{1,0:T(1,128)S(1)} %copy-done.3, s32[1,128,128]{2,1,0:T(8,128)S(1)} %copy-done.1, f32[1,3,128,128]{3,2,1,0:T(8,128)S(1)} %bitcast.9, s32[128,1]{1,0:T(8,128)S(1)} %copy.14.column_ref, s32[1,128]{1,0:T(1,128)S(1)} %copy-done.4, bf16[4,64,128]{2,1,0:T(8,128)(2,1)S(1)} %sample_early.2.refs_1_.refs_0_, ...), custom_call_target="tpu_custom_call" | custom-call | tf_op jit(solution)/shard_map/sample_last/pallas_call | solution.py:280
  12.6 23.2 %all_to_all.5 = bf16[64,4,128]{2,1,0:T(4,128)(2,1)S(1)} all-to-all(bf16[64,4,128]{2,1,0:T(4,128)(2,1)S(1)} %bitcast.10), channel_id=1, replica_groups=mesh['slab'=64,'tile'=4] {'slab'}, dimensions={0} | all-to-all | bytes 131072 | tf_op jit(solution)/shard_map/all_to_all | solution.py:359
  35.7 0.0 copy-done.2
  35.7 0.0 copy-done.6
  35.7 0.0 copy-done.5
  35.7 0.8 %composite.1 = (f32[3,1,128]{2,1,0:T(1,128)}, f32[1,128]{1,0:T(1,128)}) custom-call(bf16[256,128]{1,0:T(8,128)(2,1)S(1)} %bitcast.11, f32[1,32]{1,0:T(1,128)S(1)} %bitcast.13, f32[3,32]{1,0:T(4,128)S(1)} %copy-done.2, f32[3,1,128]{2,1,0:T(1,128)S(1)} %copy-done.5), custom_call_target="tpu_custom_call" | custom-call | tf_op jit(solution)/shard_map/composite/pallas_call | solution.py:316
Async XLA Ops:
  0.6 35.1 %copy-start.2 = (f32[3,32]{1,0:T(4,128)S(1)}, f32[3,32]{1,0:T(4,128)}, u32[]{:S(2)}) copy-start(f32[3,32]{1,0:T(4,128)} %decode_ref.3) | copy-start | bytes 1156
  0.6 7.3 %copy-start.4 = (s32[1,128]{1,0:T(1,128)S(1)}, s32[1,128]{1,0:T(1,128)}, u32[]{:S(2)}) copy-start(s32[1,128]{1,0:T(1,128)} %group_ref.1) | copy-start | bytes 1540
  0.7 7.7 %copy-start = (f32[1,128,3,128]{3,1,2,0:T(8,128)S(1)}, f32[1,128,3,128]{3,1,2,0:T(8,128)}, u32[]{:S(2)}) copy-start(f32[1,128,3,128]{3,1,2,0:T(8,128)} %param.13) | copy-start | bytes 589828
  0.7 7.7 %copy-start.1 = (s32[1,128,128]{2,1,0:T(8,128)S(1)}, s32[1,128,128]{2,1,0:T(8,128)}, u32[]{:S(2)}) copy-start(s32[1,128,128]{2,1,0:T(8,128)} %voxel_ref.5) | copy-start | bytes 196612
  0.7 7.7 %copy-start.3 = (s32[1,128]{1,0:T(1,128)S(1)}, s32[1,128]{1,0:T(1,128)}, u32[]{:S(2)}) copy-start(s32[1,128]{1,0:T(1,128)} %slot_ref.5) | copy-start | bytes 1540
  0.7 35.0 %copy-start.6 = (f32[32]{0:T(128)S(1)}, f32[32]{0:T(128)}, u32[]{:S(2)}) copy-start(f32[32]{0:T(128)} %param.17) | copy-start | bytes 388
  0.7 35.0 %copy-start.5 = (f32[3,1,128]{2,1,0:T(1,128)S(1)}, f32[3,1,128]{2,1,0:T(1,128)}, u32[]{:S(2)}) copy-start(f32[3,1,128]{2,1,0:T(1,128)} %target_ref.1) | copy-start | bytes 4612
  3.1 5.3 %collective-permute-start = (bf16[2,64,256]{2,1,0:T(8,128)(2,1)S(1)}, bf16[2,64,256]{2,1,0:T(8,128)(2,1)S(1)}, u32[]{:S(2)}, u32[]{:S(2)}) collective-permute-start(bf16[2,64,256]{2,1,0:T(8,128)(2,1)S(1)} %get-tuple-element.7), channel_id=1, source_target_pairs={{0,3},{1,2},{2,1},{3,0},{4,7},{5,6},{6,5},{7,4},{8,11},{9,10},{10,... | collective-permute-start | bytes 196616 | tf_op jit(solution)/shard_map/ppermute | solution.py:346
  6.7 3.2 %collective-permute-start.1 = (bf16[2,64,256]{2,1,0:T(8,128)(2,1)S(1)}, bf16[2,64,256]{2,1,0:T(8,128)(2,1)S(1)}, u32[]{:S(2)}, u32[]{:S(2)}) collective-permute-start(bf16[2,64,256]{2,1,0:T(8,128)(2,1)S(1)} %get-tuple-element.8), channel_id=1, source_target_pairs={{0,1},{1,0},{2,3},{3,2},{4,5},{5,4},{6,7},{7,6},{8,9},{9,8},{10,11... | collective-permute-start | bytes 196616 | tf_op jit(solution)/shard_map/ppermute | solution.py:346
  6.7 4.7 %collective-permute-start.2 = (bf16[2,64,256]{2,1,0:T(8,128)(2,1)S(1)}, bf16[2,64,256]{2,1,0:T(8,128)(2,1)S(1)}, u32[]{:S(2)}, u32[]{:S(2)}) collective-permute-start(bf16[2,64,256]{2,1,0:T(8,128)(2,1)S(1)} %get-tuple-element.9), channel_id=1, source_target_pairs={{0,2},{1,3},{2,0},{3,1},{4,6},{5,7},{6,4},{7,5},{8,10},{9,11},{10,... | collective-permute-start | bytes 196616 | tf_op jit(solution)/shard_map/ppermute | solution.py:346
